TPU v7x, 128 devices: a whole 4x4x4 slice. The times are simulated.
128 devices in a mesh: tm: 16 (over z_hi, y, core), space: 8 (over x, z_lo).
Axes of the slice: x: 4, y: 4, z: 4 (z_hi: 2, z_lo: 2; z = z_hi * 2 + z_lo), core: 2. Of those that a mesh axis runs over, the one named last changes fastest.
Arguments:
- tokens: bfloat16 [64, 24, 80, 1024], P('tm', 'space'), may hold values from -6 to 6
- w_in: bfloat16 [1024, 4416], replicated, may hold values from -0.1875 to 0.1875
- w_out: bfloat16 [2048, 1024], replicated, may hold values from -0.125 to 0.125
- a_log_time: float32 [32], replicated, may hold values from -16 to -3
- a_log_space: float32 [32], replicated, may hold values from -14 to -3
- dt_bias_time: float32 [32], replicated, may hold values from -1 to 1
- dt_bias_space: float32 [32], replicated, may hold values from -1 to 1
- skip_time: float32 [32], replicated, may hold values from 0.5 to 1.5
- skip_space: float32 [32], replicated, may hold values from 0.5 to 1.5
- norm_gain: float32 [2048], replicated, may hold values from 0.25 to 1.75
Outputs:
- mixed: bfloat16 [64, 24, 80, 1024], P('tm', 'space')
All inputs are finite; a program needn't handle non-finite values.
Results may differ from a plain program's by a relative error of at most 0.0062.
The roundings to bfloat16 on the way count: a program that leaves them out, or rounds other values in their place, can miss the bound.
Values may be sent and summed in bfloat16 or wider, within the bound.
A program may use at most 192 MiB of HBM per device.

v0:
```python
import jax
import jax.numpy as jnp
from jax import lax
from jax.sharding import PartitionSpec as P

D = 1024
HEADS = 32
HEAD_DIM = 64
STATE = 64
DI = 2048


def from_behind(value, axis, steps):
    count = lax.axis_size(axis)
    leading, last = (max(0, -steps), min(count, count - steps))
    return lax.ppermute(value, axis, [(source, source + steps) for source in range(leading, last)])


def local_scan(inner_seq, inject, readout, log_decay, step_size):
    signal = inner_seq.astype(jnp.float32)
    cum_decay = jnp.cumsum(log_decay, axis=0)
    scores = jnp.dot(readout, inject.T, preferred_element_type=jnp.float32)
    log_span = cum_decay[:, None, :] - cum_decay[None, :, :]
    length = log_decay.shape[0]
    causal = jnp.arange(length)[:, None] >= jnp.arange(length)[None, :]
    decay_mask = jnp.where(causal[:, :, None], jnp.exp(jnp.minimum(log_span, 0.0)), 0.0)
    weights = decay_mask * scores[:, :, None] * step_size[None, :, :]
    local_out = jnp.einsum("srh,rhp->shp", weights, signal, precision=lax.Precision.HIGHEST)
    tail_weight = jnp.exp(cum_decay[-1][None, :] - cum_decay) * step_size
    end_state = jnp.einsum(
        "rhp,rn->hpn",
        tail_weight[:, :, None] * signal,
        inject.astype(jnp.float32),
        precision=lax.Precision.HIGHEST,
    )
    return (local_out, end_state, cum_decay[-1], cum_decay)


def apply_start(local_out, cum_decay, readout, inner_seq, skip_gain, start_state):
    carried = jnp.einsum(
        "sn,hpn->shp", readout.astype(jnp.float32), start_state, precision=lax.Precision.HIGHEST
    )
    return (
        local_out
        + jnp.exp(cum_decay)[:, :, None] * carried
        + skip_gain[None, :, None] * inner_seq.astype(jnp.float32)
    )


def space_carry(end_state, total_decay):
    growth = jnp.exp(total_decay)[..., None, None]

    def relay_step(loop_index, start_state):
        return from_behind(growth * start_state + end_state, "space", 1)

    return lax.fori_loop(0, lax.axis_size("space") - 1, relay_step, jnp.zeros_like(end_state))


def body(
    tokens,
    w_in,
    w_out,
    a_log_time,
    a_log_space,
    dt_bias_time,
    dt_bias_space,
    skip_time,
    skip_space,
    norm_gain,
):
    base = 2 * DI
    w_time = jnp.concatenate(
        [
            w_in[:, DI:base],
            w_in[:, base : base + 2 * STATE],
            w_in[:, base + 4 * STATE : base + 4 * STATE + HEADS],
        ],
        axis=1,
    )
    w_home = jnp.concatenate(
        [
            w_in[:, :DI],
            w_in[:, base + 2 * STATE : base + 4 * STATE],
            w_in[:, base + 4 * STATE + HEADS :],
        ],
        axis=1,
    )
    fr_dev, rows_dev, cols_dev = (tokens.shape[0], tokens.shape[1], tokens.shape[2])
    n_tm = lax.axis_size("tm")
    flat_tokens = tokens.reshape(-1, D)
    home = jnp.dot(flat_tokens, w_home, preferred_element_type=jnp.float32)
    gate_z = home[:, :DI].astype(jnp.bfloat16)
    b_space = home[:, DI : DI + STATE].astype(jnp.bfloat16)
    c_space = home[:, DI + STATE : DI + 2 * STATE].astype(jnp.bfloat16)
    step_space = jax.nn.softplus(home[:, DI + 2 * STATE :] + dt_bias_space)
    decay_space = -jnp.exp(a_log_space) * step_space
    scan_all = jax.vmap(local_scan)
    time_pack = jnp.dot(flat_tokens, w_time, preferred_element_type=jnp.float32).astype(
        jnp.bfloat16
    )
    sending = time_pack.reshape(fr_dev, n_tm, -1, time_pack.shape[-1])
    time_pack = lax.all_to_all(sending, "tm", split_axis=1, concat_axis=0, tiled=True)
    frames = time_pack.shape[0]
    item_count = time_pack.shape[2]
    sequences = jnp.swapaxes(time_pack[:, 0], 0, 1)
    inner_seq = sequences[..., :DI].reshape(item_count, frames, HEADS, HEAD_DIM)
    inject = sequences[..., DI : DI + STATE]
    readout = sequences[..., DI + STATE : DI + 2 * STATE]
    raw_step = sequences[..., DI + 2 * STATE :].astype(jnp.float32)
    step_size = jax.nn.softplus(raw_step + dt_bias_time)
    log_decay = -jnp.exp(a_log_time) * step_size
    time_local_out, unused_end, unused_total, unused_cum = scan_all(
        inner_seq, inject, readout, log_decay, step_size
    )
    result = time_local_out + skip_time[None, None, :, None] * inner_seq.astype(jnp.float32)
    result = result.astype(jnp.bfloat16).reshape(item_count, frames, DI)
    returned = jnp.swapaxes(result, 0, 1)[:, None]
    time_out = lax.all_to_all(returned, "tm", split_axis=0, concat_axis=1, tiled=True)
    space_in = time_out.reshape(fr_dev, rows_dev, cols_dev, HEADS, HEAD_DIM)
    inject_grid = b_space.reshape(fr_dev, rows_dev, cols_dev, STATE)
    readout_grid = c_space.reshape(fr_dev, rows_dev, cols_dev, STATE)
    decay_grid = decay_space.reshape(fr_dev, rows_dev, cols_dev, HEADS)
    step_grid = step_space.reshape(fr_dev, rows_dev, cols_dev, HEADS)
    apply_all = jax.vmap(apply_start, in_axes=(0, 0, 0, 0, None, 0))
    state_now = jnp.zeros((fr_dev, HEADS, HEAD_DIM, STATE), jnp.float32)
    decay_sum = jnp.zeros((fr_dev, HEADS), jnp.float32)
    row_results = []
    row_offsets = []
    for row_index in range(rows_dev):
        inner_row = space_in[:, row_index]
        readout_row = readout_grid[:, row_index]
        local_out, end_state, total_decay, cum_decay = scan_all(
            inner_row,
            inject_grid[:, row_index],
            readout_row,
            decay_grid[:, row_index],
            step_grid[:, row_index],
        )
        row_results.append(
            apply_all(local_out, cum_decay, readout_row, inner_row, skip_space, state_now)
        )
        row_offsets.append(cum_decay + decay_sum[:, None, :])
        state_now = jnp.exp(total_decay)[..., None, None] * state_now + end_state
        decay_sum = decay_sum + total_decay
    space_start = space_carry(state_now, decay_sum)
    finished = []
    for row_index in range(rows_dev):
        carried = jnp.einsum(
            "fsn,fhpn->fshp",
            readout_grid[:, row_index].astype(jnp.float32),
            space_start,
            precision=lax.Precision.HIGHEST,
        )
        finished.append(
            row_results[row_index] + jnp.exp(row_offsets[row_index])[..., None] * carried
        )
    space_out = jnp.stack(finished, axis=1).reshape(-1, DI)
    gated = space_out * jax.nn.silu(gate_z.astype(jnp.float32))
    inv_scale = lax.rsqrt(jnp.mean(gated * gated, axis=-1, keepdims=True) + 1e-05)
    normed = (gated * inv_scale * norm_gain).astype(jnp.bfloat16)
    summed = jnp.dot(normed, w_out, preferred_element_type=jnp.float32) + flat_tokens.astype(
        jnp.float32
    )
    return summed.astype(jnp.bfloat16).reshape(tokens.shape)


def solution(mesh):
    placed = (P("tm", "space", None, None), P(), P(), P(), P(), P(), P(), P(), P(), P())
    return jax.shard_map(
        body, mesh=mesh, in_specs=placed, out_specs=P("tm", "space", None, None), check_vma=False
    )
```

profile of v0, /device:TPU:0, one launch (start us, length us, event | category | flops | bytes accessed | tf_op | source)
XLA Modules:
  0.0 1082.8 jit_solution(10576895644700840184)
XLA Ops:
  0.9 2.2 slice-done
  3.8 6.4 fusion.41
  10.2 7.3 reshape.156
  17.5 8.0 copy.171
  25.5 8.2 all-to-all-start
  33.8 4.6 slice.111
  38.4 54.7 %all-to-all-done = bf16[4,16,15,2208]{3,0,2,1:T(4,128)(2,1)} async-done(((bf16[4,16,15,2208]{3,0,2,1:T(4,128)(2,1)}), bf16[4,16,15,2208]{3,0,2,1:T(4,128)(2,1)}, u32[]{:S(2)}, u32[]{:S(2)}) %all-to-all-start) | async-done | bytes 4239392 | tf_op jit(solution)/shard_map/all_to_all | solution.py:102
  93.1 6.4 copy.172
  99.5 7.5 squeeze.58
  107.0 9.3 copy.173
  116.3 7.0 slice.135
  126.1 6.3 fusion.153
  132.7 20.5 %fusion = bf16[15,64,32,64]{1,3,2,0:T(8,128)(2,1)} fusion(bf16[15,64,32,64]{1,3,2,0:T(8,128)(2,1)} %bitcast.194, f32[32]{0:T(128)S(1)} %copy-done.25, f32[15,64,32]{1,2,0:T(8,128)S(1)} %get-tuple-element.43, f32[15,64,64]{2,1,0:T(8,128)S(1)} %fusion.101, f32[15,64,32]{1,2,0:T(8,128)S(1)} %copy.175, pred[64,64]{1,0:T(8,128)(4,1)S(1)} %iota_compare_fusion.1), kind=kOutput, calls=%fused_computation.2 | convolution fusion | flops 1527644160 | bytes 8360064 | tf_op jit(solution)/shard_map/vmap(srh,rhp->shp)/dot_general | solution.py:28
  153.3 10.0 copy.179
  163.3 6.5 all-to-all-start.1
  169.8 9.6 fusion.152
  188.6 3.3 fusion.99
  191.9 34.3 %all-to-all-done.1 = bf16[64,1,15,2048]{3,2,1,0:T(8,128)(2,1)} async-done(((bf16[64,1,15,2048]{3,2,1,0:T(8,128)(2,1)}), bf16[64,1,15,2048]{3,2,1,0:T(8,128)(2,1)}, u32[]{:S(2)}, u32[]{:S(2)}) %all-to-all-start.1) | async-done | bytes 3932192 | tf_op jit(solution)/shard_map/all_to_all | solution.py:118
  226.2 5.4 copy.240
  231.5 3.8 copy.181
  235.3 23.2 %reshape.159 = bf16[4,3,80,32,64]{4,3,0,2,1:T(8,128)(2,1)} reshape(bf16[4,16,1,15,2048]{4,0,3,1,2:T(4,128)(2,1)} %copy.181) | data formatting | bytes 7864320 | tf_op jit(solution)/shard_map/reshape | solution.py:119
  258.5 6.1 fusion.149
  264.6 4.3 copy.224
  268.9 5.2 copy.232
  274.1 5.2 copy.235
  279.3 2.3 fusion.53
  281.6 3.8 fusion.62
  285.4 2.7 multiply_add_fusion.2
  288.2 3.5 fusion.106
  291.7 3.9 multiply_add_fusion.1
  295.6 2.5 broadcast.70
  298.2 687.0 %while.10 = (s32[]{:T(128)}, f32[4,32,64,64]{3,2,1,0:T(8,128)}, f32[4,32,1,1]{1,0,3,2:T(4,128)S(1)}, f32[4,32,64,64]{3,2,1,0:T(8,128)}, s32[]{:T(128)}) while((s32[]{:T(128)}, f32[4,32,64,64]{3,2,1,0:T(8,128)}, f32[4,32,1,1]{1,0,3,2:T(4,128)S(1)}, f32[4,32,64,64]{3,2,1,0:T(8,128)}, s32[]{:T(128)}) %tuple.48), condition=%wide.region_5.6_spmd, body=%wide.region_4.5_spmd.sunk | while | flops 1048578 | bytes 14680677 | solution.py:56
  298.2 5.9 multiply_add_fusion.4
  304.1 4.9 collective-permute-start
  309.0 88.2 %collective-permute-done = f32[4,32,64,64]{3,2,1,0:T(8,128)} collective-permute-done((f32[4,32,64,64]{3,2,1,0:T(8,128)}, f32[4,32,64,64]{3,2,1,0:T(8,128)}, u32[]{:S(2)}, u32[]{:S(2)}) %collective-permute-start) | collective-permute-done | bytes 2097184 | tf_op jit(solution)/shard_map/while/body/eval_jaxpr/ppermute | solution.py:16
  397.2 5.9 multiply_add_fusion.4
  403.1 6.4 collective-permute-start
  409.5 87.3 %collective-permute-done = f32[4,32,64,64]{3,2,1,0:T(8,128)} collective-permute-done((f32[4,32,64,64]{3,2,1,0:T(8,128)}, f32[4,32,64,64]{3,2,1,0:T(8,128)}, u32[]{:S(2)}, u32[]{:S(2)}) %collective-permute-start) | collective-permute-done | bytes 2097184 | tf_op jit(solution)/shard_map/while/body/eval_jaxpr/ppermute | solution.py:16
  496.9 5.9 multiply_add_fusion.4
  502.8 6.8 collective-permute-start
  509.5 86.4 %collective-permute-done = f32[4,32,64,64]{3,2,1,0:T(8,128)} collective-permute-done((f32[4,32,64,64]{3,2,1,0:T(8,128)}, f32[4,32,64,64]{3,2,1,0:T(8,128)}, u32[]{:S(2)}, u32[]{:S(2)}) %collective-permute-start) | collective-permute-done | bytes 2097184 | tf_op jit(solution)/shard_map/while/body/eval_jaxpr/ppermute | solution.py:16
  595.9 5.9 multiply_add_fusion.4
  601.9 7.3 collective-permute-start
  609.2 85.5 %collective-permute-done = f32[4,32,64,64]{3,2,1,0:T(8,128)} collective-permute-done((f32[4,32,64,64]{3,2,1,0:T(8,128)}, f32[4,32,64,64]{3,2,1,0:T(8,128)}, u32[]{:S(2)}, u32[]{:S(2)}) %collective-permute-start) | collective-permute-done | bytes 2097184 | tf_op jit(solution)/shard_map/while/body/eval_jaxpr/ppermute | solution.py:16
  694.6 5.9 multiply_add_fusion.4
  700.6 7.3 collective-permute-start
  707.9 84.6 %collective-permute-done = f32[4,32,64,64]{3,2,1,0:T(8,128)} collective-permute-done((f32[4,32,64,64]{3,2,1,0:T(8,128)}, f32[4,32,64,64]{3,2,1,0:T(8,128)}, u32[]{:S(2)}, u32[]{:S(2)}) %collective-permute-start) | collective-permute-done | bytes 2097184 | tf_op jit(solution)/shard_map/while/body/eval_jaxpr/ppermute | solution.py:16
  792.4 5.9 multiply_add_fusion.4
  798.3 7.3 collective-permute-start
  805.6 83.6 %collective-permute-done = f32[4,32,64,64]{3,2,1,0:T(8,128)} collective-permute-done((f32[4,32,64,64]{3,2,1,0:T(8,128)}, f32[4,32,64,64]{3,2,1,0:T(8,128)}, u32[]{:S(2)}, u32[]{:S(2)}) %collective-permute-start) | collective-permute-done | bytes 2097184 | tf_op jit(solution)/shard_map/while/body/eval_jaxpr/ppermute | solution.py:16
  889.3 5.9 multiply_add_fusion.4
  895.2 7.3 collective-permute-start
  902.5 82.7 %collective-permute-done = f32[4,32,64,64]{3,2,1,0:T(8,128)} collective-permute-done((f32[4,32,64,64]{3,2,1,0:T(8,128)}, f32[4,32,64,64]{3,2,1,0:T(8,128)}, u32[]{:S(2)}, u32[]{:S(2)}) %collective-permute-start) | collective-permute-done | bytes 2097184 | tf_op jit(solution)/shard_map/while/body/eval_jaxpr/ppermute | solution.py:16
  985.2 4.0 fusion.111
  989.2 4.2 fusion.104
  993.5 5.6 fusion.34
  999.1 7.6 fusion.52
  1006.8 7.8 fusion.57
  1014.7 8.1 fusion.61
  1022.9 10.6 pad_maximum_fusion
  1033.4 18.0 %copy.214 = f32[4,3,80,32,64]{4,3,2,1,0:T(8,128)} copy(f32[4,3,80,32,64]{2,4,3,0,1:T(8,128)} %pad_maximum_fusion) | data formatting | bytes 15728640 | tf_op jit(solution)/shard_map/stack | solution.py:157
  1051.4 14.5 %reshape.164 = f32[960,2048]{1,0:T(8,128)} reshape(f32[4,3,80,32,64]{4,3,2,1,0:T(8,128)} %copy.214) | data formatting | bytes 15728640 | tf_op jit(solution)/shard_map/reshape | solution.py:157
  1065.9 5.8 multiply_reduce_fusion
  1073.1 9.3 add_convert_fusion
  (94 shorter events, 15.1 us)
Async XLA Ops:
  0.9 2.3 slice-start
  0.9 2.9 copy-start.20
  25.5 67.6 %all-to-all-start = ((bf16[4,16,15,2208]{3,0,2,1:T(4,128)(2,1)}), bf16[4,16,15,2208]{3,0,2,1:T(4,128)(2,1)}, u32[]{:S(2)}, u32[]{:S(2)}) async-start(bf16[4,16,15,2208]{3,0,2,1:T(4,128)(2,1)} %copy.171), calls=%async_computation | async-start | bytes 8847360 | tf_op jit(solution)/shard_map/all_to_all | solution.py:102
  33.8 4.6 copy-start.23
  33.8 4.6 copy-start.24
  116.3 8.4 copy-start.19
  116.3 16.4 %copy-start.25 = (f32[32]{0:T(128)S(1)}, f32[32]{0:T(128)}, u32[]{:S(2)}) copy-start(f32[32]{0:T(128)} %param.19) | copy-start | bytes 388
  163.3 6.5 slice-start.1
  163.3 62.9 %all-to-all-start.1 = ((bf16[64,1,15,2048]{3,2,1,0:T(8,128)(2,1)}), bf16[64,1,15,2048]{3,2,1,0:T(8,128)(2,1)}, u32[]{:S(2)}, u32[]{:S(2)}) async-start(bf16[64,1,15,2048]{3,2,1,0:T(8,128)(2,1)} %bitcast.192), calls=%async_computation.1 | async-start | bytes 8388608 | tf_op jit(solution)/shard_map/all_to_all | solution.py:118
  169.8 9.6 copy-start.18
  281.6 3.8 copy-start.3
  288.1 3.6 copy-start.5
  304.1 93.1 %collective-permute-start = (f32[4,32,64,64]{3,2,1,0:T(8,128)}, f32[4,32,64,64]{3,2,1,0:T(8,128)}, u32[]{:S(2)}, u32[]{:S(2)}) collective-permute-start(f32[4,32,64,64]{3,2,1,0:T(8,128)} %multiply_add_fusion.4), channel_id=1, source_target_pairs={{0,1},{1,2},{2,3},{3,4},{4,5},{5,6},{6,7},{8,9},{9,10},{10,11},{11... | collective-permute-start | bytes 6291464 | tf_op jit(solution)/shard_map/while/body/eval_jaxpr/ppermute | solution.py:16
  403.1 93.7 %collective-permute-start = (f32[4,32,64,64]{3,2,1,0:T(8,128)}, f32[4,32,64,64]{3,2,1,0:T(8,128)}, u32[]{:S(2)}, u32[]{:S(2)}) collective-permute-start(f32[4,32,64,64]{3,2,1,0:T(8,128)} %multiply_add_fusion.4), channel_id=1, source_target_pairs={{0,1},{1,2},{2,3},{3,4},{4,5},{5,6},{6,7},{8,9},{9,10},{10,11},{11... | collective-permute-start | bytes 6291464 | tf_op jit(solution)/shard_map/while/body/eval_jaxpr/ppermute | solution.py:16
  502.8 93.2 %collective-permute-start = (f32[4,32,64,64]{3,2,1,0:T(8,128)}, f32[4,32,64,64]{3,2,1,0:T(8,128)}, u32[]{:S(2)}, u32[]{:S(2)}) collective-permute-start(f32[4,32,64,64]{3,2,1,0:T(8,128)} %multiply_add_fusion.4), channel_id=1, source_target_pairs={{0,1},{1,2},{2,3},{3,4},{4,5},{5,6},{6,7},{8,9},{9,10},{10,11},{11... | collective-permute-start | bytes 6291464 | tf_op jit(solution)/shard_map/while/body/eval_jaxpr/ppermute | solution.py:16
  601.9 92.8 %collective-permute-start = (f32[4,32,64,64]{3,2,1,0:T(8,128)}, f32[4,32,64,64]{3,2,1,0:T(8,128)}, u32[]{:S(2)}, u32[]{:S(2)}) collective-permute-start(f32[4,32,64,64]{3,2,1,0:T(8,128)} %multiply_add_fusion.4), channel_id=1, source_target_pairs={{0,1},{1,2},{2,3},{3,4},{4,5},{5,6},{6,7},{8,9},{9,10},{10,11},{11... | collective-permute-start | bytes 6291464 | tf_op jit(solution)/shard_map/while/body/eval_jaxpr/ppermute | solution.py:16
  700.6 91.9 %collective-permute-start = (f32[4,32,64,64]{3,2,1,0:T(8,128)}, f32[4,32,64,64]{3,2,1,0:T(8,128)}, u32[]{:S(2)}, u32[]{:S(2)}) collective-permute-start(f32[4,32,64,64]{3,2,1,0:T(8,128)} %multiply_add_fusion.4), channel_id=1, source_target_pairs={{0,1},{1,2},{2,3},{3,4},{4,5},{5,6},{6,7},{8,9},{9,10},{10,11},{11... | collective-permute-start | bytes 6291464 | tf_op jit(solution)/shard_map/while/body/eval_jaxpr/ppermute | solution.py:16
  798.3 90.9 %collective-permute-start = (f32[4,32,64,64]{3,2,1,0:T(8,128)}, f32[4,32,64,64]{3,2,1,0:T(8,128)}, u32[]{:S(2)}, u32[]{:S(2)}) collective-permute-start(f32[4,32,64,64]{3,2,1,0:T(8,128)} %multiply_add_fusion.4), channel_id=1, source_target_pairs={{0,1},{1,2},{2,3},{3,4},{4,5},{5,6},{6,7},{8,9},{9,10},{10,11},{11... | collective-permute-start | bytes 6291464 | tf_op jit(solution)/shard_map/while/body/eval_jaxpr/ppermute | solution.py:16
  895.2 90.0 %collective-permute-start = (f32[4,32,64,64]{3,2,1,0:T(8,128)}, f32[4,32,64,64]{3,2,1,0:T(8,128)}, u32[]{:S(2)}, u32[]{:S(2)}) collective-permute-start(f32[4,32,64,64]{3,2,1,0:T(8,128)} %multiply_add_fusion.4), channel_id=1, source_target_pairs={{0,1},{1,2},{2,3},{3,4},{4,5},{5,6},{6,7},{8,9},{9,10},{10,11},{11... | collective-permute-start | bytes 6291464 | tf_op jit(solution)/shard_map/while/body/eval_jaxpr/ppermute | solution.py:16
  989.2 4.3 copy-start.15
  989.2 4.3 copy-start.16
  993.5 5.6 copy-start.1
  993.5 5.6 copy-start.17
  999.1 7.7 copy-start.4
  999.1 7.7 copy-start.7
  999.1 7.7 copy-start.11
  999.1 7.7 copy-start.12
  999.1 7.7 copy-start.14
  1006.8 7.9 copy-start.6
  1006.8 7.9 copy-start.8
  1006.8 7.9 copy-start.9
  1006.8 7.9 copy-start.10
  1006.8 7.9 copy-start.13
  1014.7 8.1 copy-start.2
  1065.9 6.7 copy-start
  1065.9 7.2 copy-start.21
  1065.9 7.2 copy-start.22
where the time goes:
time: 1100 us; the launch traced here: 1080 us
  waiting for transfers between devices  687 us (62%)
  local copies, waits for them, and re-layouts  161 us (15%)
  matrix products  105 us (10%)
  other arithmetic  66.9 us (6%)
  starting transfers between devices  62.1 us (6%)
    ppermute x7, waiting for transfers between devices, from_behind(): lax.ppermute(value, axis, [(source, source + steps) for source in range(l...  598 us
    all_to_all x1, waiting for transfers between devices, body(): lax.all_to_all(sending, 'tm', split_axis=1, concat_axis=0, tiled=True)  54.7 us
    ppermute x7, starting transfers between devices, from_behind(): lax.ppermute(value, axis, [(source, source + steps) for source in range(l...  47.3 us
    dot_general x4, matrix products, local_scan(): jnp.einsum('srh,rhp->shp', weights, signal, precision=lax.Precision.HIGHEST)  42.1 us
    add x7, other arithmetic, relay_step(): return from_behind(growth * start_state + end_state, 'space', 1)  41.3 us
    all_to_all x1, waiting for transfers between devices, body(): lax.all_to_all(returned, 'tm', split_axis=0, concat_axis=1, tiled=True)  34.3 us
    reshape x1, local copies, waits for them, and re-layouts, body(): space_in = time_out.reshape(fr_dev, rows_dev, cols_dev, HEADS, HEAD_DIM)  23.2 us
  transfers between devices with their start and end apart: 9, of which 9 were waited for; matrix products, arithmetic and copies ran while one was open for 2% of the time, Pallas kernels for 0%

commit v1 on v0

v1 whole, which is shorter than its diff:
```python
import functools

import jax
import jax.numpy as jnp
from jax import lax
from jax.experimental import pallas as pl
from jax.experimental.pallas import tpu as pltpu
from jax.sharding import PartitionSpec as P

D = 1024
HEADS = 32
HEAD_DIM = 64
STATE = 64
DI = 2048
CHUNK = 64
F32 = jnp.float32
BF16 = jnp.bfloat16
MIB = 1 << 20


def mm(a, b):
    return jnp.dot(a, b, preferred_element_type=F32)


def softplus(v):
    return jnp.maximum(v, 0.0) + jnp.log1p(jnp.exp(-jnp.abs(v)))


def split3(v):
    hi = v.astype(BF16)
    rest = v - hi.astype(F32)
    mid = rest.astype(BF16)
    low = (rest - mid.astype(F32)).astype(BF16)
    return jnp.concatenate([hi, mid, low], axis=1)


def head_spread():
    row = lax.broadcasted_iota(jnp.int32, (3 * HEADS, DI), 0) % HEADS
    col = lax.broadcasted_iota(jnp.int32, (3 * HEADS, DI), 1) // HEAD_DIM
    return (row == col).astype(BF16)


def causal_ones():
    row = lax.broadcasted_iota(jnp.int32, (CHUNK, CHUNK), 0)
    col = lax.broadcasted_iota(jnp.int32, (CHUNK, CHUNK), 1)
    return row >= col


def chunk_cumsum(log_decay):
    tri = causal_ones().astype(F32).astype(BF16)
    wide = mm(tri, split3(log_decay))
    return wide[:, :HEADS] + wide[:, HEADS : 2 * HEADS] + wide[:, 2 * HEADS :]


def row_forms(cum, step):
    pair = jnp.concatenate([cum, step, jnp.zeros((CHUNK, 2 * HEADS), F32)], axis=1)
    return jnp.concatenate([pair, pair], axis=0).T


def pair_rows(turned_ref, base, j, lane_low):
    even = turned_ref[pl.ds(base + 2 * j, 1), :]
    odd = turned_ref[pl.ds(base + 2 * j + 1, 1), :]
    return jnp.where(lane_low, even, odd)


def decay_weights(cum_wide, turned_ref, scores2, j, lane_low):
    cum_row = pair_rows(turned_ref, 0, j, lane_low)
    step_row = pair_rows(turned_ref, HEADS, j, lane_low)
    span = jnp.exp(jnp.minimum(cum_wide - cum_row, 0.0))
    return (span * (scores2 * step_row)).astype(BF16)


def masked_scores(readout, inject):
    scores = lax.dot_general(readout, inject, (((1,), (1,)), ((), ())), preferred_element_type=F32)
    scores = jnp.where(causal_ones(), scores, 0.0)
    return jnp.concatenate([scores, scores], axis=1)


def block_pair(x_pair):
    low = lax.broadcasted_iota(jnp.int32, x_pair.shape, 1) < HEAD_DIM
    zero = jnp.zeros_like(x_pair)
    return jnp.concatenate([jnp.where(low, x_pair, zero), jnp.where(low, zero, x_pair)], axis=0)


def time_kernel(tok_ref, wx_ref, wt_ref, bias_ref, alog_ref, skip_ref, out_ref, spread, x_ref, small_ref, cum_ref, turned):
    items = tok_ref.shape[0] // CHUNK

    @pl.when(pl.program_id(0) == 0)
    def _():
        spread[...] = head_spread()

    tok = tok_ref[...]
    x_ref[...] = mm(tok, wx_ref[...]).astype(BF16)
    small_ref[...] = mm(tok, wt_ref[...]).astype(BF16)
    lane_low = lax.broadcasted_iota(jnp.int32, (1, 2 * CHUNK), 1) < CHUNK
    rate = -jnp.exp(alog_ref[...])

    def item(index, carry):
        rows = pl.ds(pl.multiple_of(index * CHUNK, CHUNK), CHUNK)
        small = small_ref[rows, :]
        scores2 = masked_scores(small[:, STATE : 2 * STATE], small[:, :STATE])
        step = softplus(small[:, 4 * STATE : 4 * STATE + HEADS].astype(F32) + bias_ref[...])
        cum = chunk_cumsum(rate * step)
        turned[...] = row_forms(cum, step)
        cum_ref[...] = mm(split3(cum), spread[...])
        for j in range(HEADS // 2):
            lanes = pl.ds(j * 128, 128)
            weights = decay_weights(cum_ref[:, lanes], turned, scores2, j, lane_low)
            x_pair = x_ref[rows, lanes]
            local = mm(weights, block_pair(x_pair))
            out_ref[rows, lanes] = (local + skip_ref[:, lanes] * x_pair.astype(F32)).astype(BF16)
        return carry

    lax.fori_loop(0, items, item, 0)


def time_scan(tok, w_in, w_tail, bias, alog, skip_wide, per_step):
    rows = per_step * CHUNK
    total = tok.shape[0]
    whole = lambda shape: pl.BlockSpec(shape, lambda i: (0, 0), pipeline_mode=pl.Buffered(1))
    return pl.pallas_call(
        time_kernel,
        out_shape=jax.ShapeDtypeStruct((total, DI), BF16),
        grid=(total // rows,),
        in_specs=[
            pl.BlockSpec((rows, D), lambda i: (i, 0)),
            pl.BlockSpec((D, DI), lambda i: (0, 1), pipeline_mode=pl.Buffered(1)),
            whole(w_tail.shape),
            whole((1, HEADS)),
            whole((1, HEADS)),
            whole((1, DI)),
        ],
        out_specs=pl.BlockSpec((rows, DI), lambda i: (i, 0)),
        scratch_shapes=[
            pltpu.VMEM((3 * HEADS, DI), BF16),
            pltpu.VMEM((rows, DI), BF16),
            pltpu.VMEM((rows, w_tail.shape[1]), BF16),
            pltpu.VMEM((CHUNK, DI), F32),
            pltpu.VMEM((128, 128), F32),
        ],
        compiler_params=pltpu.CompilerParams(vmem_limit_bytes=40 * MIB),
        cost_estimate=pl.CostEstimate(
            flops=2 * total * D * 2400 + 2 * total * 128 * DI,
            bytes_accessed=2 * total * (D + DI) + 2 * D * 2400,
            transcendentals=total * DI,
        ),
    )(tok, w_in, w_tail, bias, alog, skip_wide)


def home_kernel(tok_ref, wz_ref, wt_ref, bias_ref, alog_ref, z_ref, w_ref, small_ref, decay_ref, spread, cum_ref, turned):
    seq = tok_ref.shape[0]

    @pl.when(pl.program_id(0) == 0)
    def _():
        spread[...] = head_spread()

    tok = tok_ref[...]
    z_ref[...] = mm(tok, wz_ref[...]).astype(BF16)
    tail = mm(tok, wt_ref[...])
    inject = tail[:, 2 * STATE : 3 * STATE].astype(BF16)
    readout = tail[:, 3 * STATE : 4 * STATE].astype(BF16)
    step = softplus(tail[:, 4 * STATE + HEADS : 4 * STATE + 2 * HEADS] + bias_ref[...])
    pad = w_ref.shape[0] - seq
    inject = jnp.concatenate([inject, jnp.zeros((pad, STATE), BF16)], axis=0)
    readout = jnp.concatenate([readout, jnp.zeros((pad, STATE), BF16)], axis=0)
    step = jnp.concatenate([step, jnp.zeros((pad, HEADS), F32)], axis=0)
    small_ref[...] = jnp.concatenate([inject, readout], axis=1)
    log_decay = -jnp.exp(alog_ref[...]) * step
    lane_low = lax.broadcasted_iota(jnp.int32, (1, 2 * CHUNK), 1) < CHUNK
    for k in range(w_ref.shape[0] // CHUNK):
        rows = pl.ds(k * CHUNK, CHUNK)
        part = slice(k * CHUNK, (k + 1) * CHUNK)
        cum = chunk_cumsum(log_decay[part])
        decay_ref[rows, :] = jnp.concatenate(
            [cum, step[part], jnp.zeros((CHUNK, 2 * HEADS), F32)], axis=1
        )
        turned[k] = row_forms(cum, step[part])
        cum_ref[...] = mm(split3(cum), spread[...])
        scores2 = masked_scores(readout[part], inject[part])
        for j in range(HEADS // 2):
            lanes = pl.ds(j * 128, 128)
            w_ref[rows, lanes] = decay_weights(cum_ref[:, lanes], turned.at[k], scores2, j, lane_low)


def home_part(tok, w_in, w_tail, bias, alog, frames):
    total = tok.shape[0]
    seq = total // frames
    padded = -(-seq // CHUNK) * CHUNK
    whole = lambda shape: pl.BlockSpec(shape, lambda i: (0, 0), pipeline_mode=pl.Buffered(1))
    row = lambda n, width: pl.BlockSpec((n, width), lambda i: (i, 0))
    return pl.pallas_call(
        home_kernel,
        out_shape=(
            jax.ShapeDtypeStruct((total, DI), BF16),
            jax.ShapeDtypeStruct((frames * padded, DI), BF16),
            jax.ShapeDtypeStruct((frames * padded, 2 * STATE), BF16),
            jax.ShapeDtypeStruct((frames * padded, 128), F32),
        ),
        grid=(frames,),
        in_specs=[
            row(seq, D),
            whole((D, DI)),
            whole(w_tail.shape),
            whole((1, HEADS)),
            whole((1, HEADS)),
        ],
        out_specs=(row(seq, DI), row(padded, DI), row(padded, 2 * STATE), row(padded, 128)),
        scratch_shapes=[
            pltpu.VMEM((3 * HEADS, DI), BF16),
            pltpu.VMEM((CHUNK, DI), F32),
            pltpu.VMEM((padded // CHUNK, 128, 128), F32),
        ],
        compiler_params=pltpu.CompilerParams(vmem_limit_bytes=40 * MIB),
        cost_estimate=pl.CostEstimate(
            flops=2 * total * D * 2400,
            bytes_accessed=2 * total * (D + 2 * DI) + 2 * D * 2400,
            transcendentals=total * DI,
        ),
    )(tok, w_in, w_tail, bias, alog)


def spread_last(cum, spread):
    last = jnp.broadcast_to(jnp.exp(cum[CHUNK - 1 : CHUNK, :]), (16, HEADS))
    return mm(split3(last), spread)[:1]


def state_kernel(x_ref, small_ref, decay_ref, starts_ref, end_ref, spread):
    seq = x_ref.shape[0]

    @pl.when(pl.program_id(0) == 0)
    def _():
        spread[...] = head_spread()

    state = jnp.zeros((STATE, DI), F32)
    count = starts_ref.shape[0] // STATE
    for k in range(count):
        size = min(CHUNK, seq - k * CHUNK)
        starts_ref[pl.ds(k * STATE, STATE), :] = state.astype(BF16)
        decay = decay_ref[pl.ds(k * CHUNK, CHUNK), :]
        cum, step = decay[:, :HEADS], decay[:, HEADS : 2 * HEADS]
        tail = (jnp.exp(cum[CHUNK - 1 :, :] - cum) * step)[:size]
        tail_wide = mm(split3(tail)[:, : 2 * HEADS], spread[: 2 * HEADS, :])
        x = x_ref[pl.ds(k * CHUNK, size), :].astype(F32)
        weighted = (x * tail_wide).astype(BF16)
        inject = small_ref[pl.ds(k * CHUNK, size), :STATE]
        added = lax.dot_general(inject, weighted, (((0,), (0,)), ((), ())), preferred_element_type=F32)
        state = spread_last(cum, spread[...]) * state + added
    end_ref[...] = state.astype(BF16)


def space_states(x, small, decay, frames):
    total = x.shape[0]
    seq = total // frames
    padded = decay.shape[0] // frames
    count = padded // CHUNK
    row = lambda n, width: pl.BlockSpec((n, width), lambda i: (i, 0))
    return pl.pallas_call(
        state_kernel,
        out_shape=(
            jax.ShapeDtypeStruct((frames * count * STATE, DI), BF16),
            jax.ShapeDtypeStruct((frames * STATE, DI), BF16),
        ),
        grid=(frames,),
        in_specs=[row(seq, DI), row(padded, 2 * STATE), row(padded, 128)],
        out_specs=(row(count * STATE, DI), row(STATE, DI)),
        scratch_shapes=[pltpu.VMEM((3 * HEADS, DI), BF16)],
        compiler_params=pltpu.CompilerParams(vmem_limit_bytes=32 * MIB),
        cost_estimate=pl.CostEstimate(
            flops=2 * total * 128 * DI, bytes_accessed=4 * total * DI, transcendentals=0
        ),
    )(x, small, decay)


def local_kernel(x_ref, w_ref, skip_ref, out_ref):
    seq = x_ref.shape[0]
    for k in range(w_ref.shape[0] // CHUNK):
        size = min(CHUNK, seq - k * CHUNK)
        rows = pl.ds(k * CHUNK, size)
        for j in range(HEADS // 2):
            lanes = pl.ds(j * 128, 128)
            x_pair = x_ref[rows, lanes]
            padded = x_pair
            if size < CHUNK:
                padded = jnp.concatenate([x_pair, jnp.zeros((CHUNK - size, 128), BF16)], axis=0)
            local = mm(w_ref[rows, lanes], block_pair(padded))
            out_ref[rows, lanes] = local + skip_ref[:, lanes] * x_pair.astype(F32)


def space_local(x, weights, skip_wide, frames):
    total = x.shape[0]
    seq = total // frames
    padded = weights.shape[0] // frames
    row = lambda n, width: pl.BlockSpec((n, width), lambda i: (i, 0))
    return pl.pallas_call(
        local_kernel,
        out_shape=jax.ShapeDtypeStruct((total, DI), F32),
        grid=(frames,),
        in_specs=[
            row(seq, DI),
            row(padded, DI),
            pl.BlockSpec((1, DI), lambda i: (0, 0), pipeline_mode=pl.Buffered(1)),
        ],
        out_specs=row(seq, DI),
        compiler_params=pltpu.CompilerParams(vmem_limit_bytes=32 * MIB),
        cost_estimate=pl.CostEstimate(
            flops=2 * total * 128 * DI, bytes_accessed=8 * total * DI, transcendentals=0
        ),
    )(x, weights, skip_wide)


def finish_kernel(local_ref, z_ref, small_ref, decay_ref, starts_ref, from_ref, gain_ref, wo_ref, tok_ref, out_ref, spread, y_ref):
    seq = local_ref.shape[0]

    @pl.when(pl.program_id(0) == 0)
    def _():
        spread[...] = head_spread()

    offset = jnp.zeros((1, HEADS), F32)
    entering = from_ref[...].astype(F32)
    for k in range(decay_ref.shape[0] // CHUNK):
        size = min(CHUNK, seq - k * CHUNK)
        rows = pl.ds(k * CHUNK, size)
        cum = decay_ref[pl.ds(k * CHUNK, CHUNK), :HEADS]
        reach = mm(split3(jnp.broadcast_to(jnp.exp(offset), (16, HEADS))), spread[...])[:1]
        offset = offset + cum[CHUNK - 1 :, :]
        state = (starts_ref[pl.ds(k * STATE, STATE), :].astype(F32) + reach * entering).astype(BF16)
        carried = mm(small_ref[rows, STATE:], state)
        grown = mm(split3(jnp.exp(cum[:size])), spread[...])
        z = z_ref[rows, :].astype(F32)
        y = (local_ref[rows, :] + grown * carried) * (z * (1.0 / (1.0 + jnp.exp(-z))))
        scale = lax.rsqrt(jnp.mean(y * y, axis=1, keepdims=True) + 1e-5)
        y_ref[rows, :] = (y * scale * gain_ref[...]).astype(BF16)
    out_ref[...] = (mm(y_ref[...], wo_ref[...]) + tok_ref[...].astype(F32)).astype(BF16)


def finish(local, z, small, decay, starts, entering, gain, w_out, tok, frames):
    total = local.shape[0]
    seq = total // frames
    padded = decay.shape[0] // frames
    count = padded // CHUNK
    whole = lambda shape: pl.BlockSpec(shape, lambda i: (0, 0), pipeline_mode=pl.Buffered(1))
    row = lambda n, width: pl.BlockSpec((n, width), lambda i: (i, 0))
    return pl.pallas_call(
        finish_kernel,
        out_shape=jax.ShapeDtypeStruct((total, D), BF16),
        grid=(frames,),
        in_specs=[
            row(seq, DI),
            row(seq, DI),
            row(padded, 2 * STATE),
            row(padded, 128),
            row(count * STATE, DI),
            row(STATE, DI),
            whole((1, DI)),
            whole((DI, D)),
            row(seq, D),
        ],
        out_specs=row(seq, D),
        scratch_shapes=[pltpu.VMEM((3 * HEADS, DI), BF16), pltpu.VMEM((seq, DI), BF16)],
        compiler_params=pltpu.CompilerParams(vmem_limit_bytes=48 * MIB),
        cost_estimate=pl.CostEstimate(
            flops=2 * total * (D + 64) * DI, bytes_accessed=8 * total * DI, transcendentals=total * DI
        ),
    )(local, z, small, decay, starts, entering, gain, w_out, tok)


def space_exchange(end, totals):
    n = lax.axis_size("space")
    frames = totals.shape[0]
    part = end.shape[0] // n
    per_frame = STATE // part
    growth = jnp.exp(lax.all_gather(totals, "space"))
    mine = lax.axis_index("space") // per_frame
    growth = lax.dynamic_index_in_dim(growth, mine, axis=1, keepdims=False)
    growth = jnp.repeat(growth, HEAD_DIM, axis=1)[:, None, :]
    got = lax.all_to_all(end.reshape(n, part, DI), "space", 0, 0, tiled=True)
    running = jnp.zeros((part, DI), F32)
    starts = []
    for device in range(n):
        starts.append(running.astype(BF16))
        running = growth[device] * running + got[device].astype(F32)
    back = lax.all_to_all(jnp.stack(starts), "space", 0, 0, tiled=True)
    return back.reshape(frames * STATE, DI)


def body(
    tokens,
    w_in,
    w_out,
    a_log_time,
    a_log_space,
    dt_bias_time,
    dt_bias_space,
    skip_time,
    skip_space,
    norm_gain,
):
    frames = tokens.shape[0]
    n_tm = lax.axis_size("tm")
    flat = tokens.reshape(-1, D)
    seq = flat.shape[0] // frames
    items = seq // n_tm
    w_tail = w_in[:, 2 * DI :]
    one = lambda v: v.reshape(1, -1)
    wide = lambda v: jnp.repeat(v, HEAD_DIM).reshape(1, DI)

    got = lax.all_to_all(tokens.reshape(frames, n_tm, items, D), "tm", 1, 0, tiled=True)
    time_tok = jnp.swapaxes(got[:, 0], 0, 1).reshape(-1, D)
    gate, weights, small, decay = home_part(
        flat, w_in, w_tail, one(dt_bias_space), one(a_log_space), frames
    )
    time_out = time_scan(time_tok, w_in, w_tail, one(dt_bias_time), one(a_log_time), wide(skip_time), 5)
    returned = jnp.swapaxes(time_out.reshape(items, n_tm * frames, DI), 0, 1)[:, None]
    time_out = lax.all_to_all(returned, "tm", 0, 1, tiled=True).reshape(-1, DI)

    totals = decay.reshape(frames, -1, CHUNK, 128)[:, :, CHUNK - 1, :HEADS].sum(axis=1)
    starts, end = space_states(time_out, small, decay, frames)
    entering = space_exchange(end, totals)
    local = space_local(time_out, weights, wide(skip_space), frames)
    out = finish(local, gate, small, decay, starts, entering, one(norm_gain), w_out, flat, frames)
    return out.reshape(tokens.shape)


def solution(mesh):
    placed = (P("tm", "space", None, None), P(), P(), P(), P(), P(), P(), P(), P(), P())
    return jax.shard_map(
        body, mesh=mesh, in_specs=placed, out_specs=P("tm", "space", None, None), check_vma=False
    )
```

time: 1100 us -> 257 us (0.23); the launches traced: 1080 us -> 254 us
  waiting for transfers between devices: 687 us -> 50.1 us
  matrix products: 105 us -> 0 us
  local copies, waits for them, and re-layouts: 161 us -> 77.9 us
  Pallas kernels: 0 us -> 62.2 us
  other arithmetic: 66.9 us -> 9.25 us
  starting transfers between devices: 62.1 us -> 21.4 us
  blocking collectives: 0 us -> 32.7 us
    ppermute x7 -> x0, waiting for transfers between devices: 598 us -> none  [from_behind(): lax.ppermute(value, axis, [(source, source + steps) for source in range(l...]
    dot_general x20 -> x0, matrix products: 105 us -> none  [the longest x4 42.1 us: local_scan(): jnp.einsum('srh,rhp->shp', weights, signal, precision=lax.Precision.HIGHEST)]
    pallas_call x0 -> x5, Pallas kernels: none -> 62.2 us  [the longest x1 20.8 us: time_scan(): pl.pallas_call(time_kernel, out_shape=jax.ShapeDtypeStruct((total, DI), B...]
    reshape x5 -> x2, local copies, waits for them, and re-layouts: 62.9 us -> 9.24 us  [the longest x1 5.15 us: body(): time_out = lax.all_to_all(returned, 'tm', 0, 1, tiled=True).reshape(-1, DI)]
    ppermute x7 -> x0, starting transfers between devices: 47.3 us -> none  [from_behind(): lax.ppermute(value, axis, [(source, source + steps) for source in range(l...]
    add x7 -> x0, other arithmetic: 41.3 us -> none  [relay_step(): return from_behind(growth * start_state + end_state, 'space', 1)]
    all_to_all x2 -> x4, waiting for transfers between devices: 89 us -> 50.1 us  [the longest x1 35.6 us: body(): time_out = lax.all_to_all(returned, 'tm', 0, 1, tiled=True).reshape(-1, DI)]
    all_gather x0 -> x1, blocking collectives: none -> 32.7 us  [space_exchange(): growth = jnp.exp(lax.all_gather(totals, 'space'))]
  transfers between devices with their start and end apart: 9 -> 4, of which waited for: 9 -> 2; matrix products, arithmetic and copies ran while one was open for 2% -> 13% of each run, Pallas kernels for 0% -> 8%
where the time goes in v1:
time: 257 us; the launch traced here: 254 us
  local copies, waits for them, and re-layouts  77.9 us (30%)
  Pallas kernels  62.2 us (24%)
  waiting for transfers between devices  50.1 us (19%)
  blocking collectives  32.7 us (13%)
  starting transfers between devices  21.4 us (8%)
  other arithmetic  9.25 us (4%)
    all_to_all x1, waiting for transfers between devices, body(): time_out = lax.all_to_all(returned, 'tm', 0, 1, tiled=True).reshape(-1, DI)  35.6 us
    unnamed x37, local copies, waits for them, and re-layouts  34.2 us
    all_gather x1, blocking collectives, space_exchange(): growth = jnp.exp(lax.all_gather(totals, 'space'))  32.7 us
    pallas_call x1, Pallas kernels, time_scan(): pl.pallas_call(time_kernel, out_shape=jax.ShapeDtypeStruct((total, DI), B...  20.8 us
    pallas_call x1, Pallas kernels, home_part(): pl.pallas_call(home_kernel, out_shape=(jax.ShapeDtypeStruct((total, DI),...  16.6 us
    pallas_call x1, Pallas kernels, finish(): pl.pallas_call(finish_kernel, out_shape=jax.ShapeDtypeStruct((total, D),...  16.3 us
    broadcast_in_dim x13, local copies, waits for them, and re-layouts, space_exchange(): growth = jnp.repeat(growth, HEAD_DIM, axis=1)[:, None, :]  15.5 us
    all_to_all x1, waiting for transfers between devices, body(): lax.all_to_all(tokens.reshape(frames, n_tm, items, D), 'tm', 1, 0, tiled=...  14.5 us
  transfers between devices with their start and end apart: 4, of which 2 were waited for; matrix products, arithmetic and copies ran while one was open for 13% of the time, Pallas kernels for 8%

profile of v1, /device:TPU:0, one launch (start us, length us, event | category | flops | bytes accessed | tf_op | source)
XLA Modules:
  0.0 253.8 jit_solution(7268506010597145445)
XLA Ops:
  0.0 4.3 %copy.26 = bf16[4,3,80,1024]{3,0,2,1:T(4,128)(2,1)} copy(bf16[4,3,80,1024]{3,2,1,0:T(8,128)(2,1)} %param.10) | data formatting | bytes 3932160 | tf_op args[0]
  4.3 8.0 %all-to-all-start = ((bf16[4,16,15,1024]{3,0,2,1:T(4,128)(2,1)}), bf16[4,16,15,1024]{3,0,2,1:T(4,128)(2,1)S(1)}, u32[]{:S(2)}, u32[]{:S(2)}) async-start(bf16[4,16,15,1024]{3,0,2,1:T(4,128)(2,1)} %bitcast.61), calls=%async_computation | async-start | bytes 3932160 | tf_op jit(solution)/shard_map/all_to_all | solution.py:407
  12.3 0.0 copy-start.16
  12.3 11.9 %copy.29.wx_ref.wz_ref = bf16[1024,4416]{1,0:T(8,128)(2,1)} copy(bf16[1024,4416]{0,1:T(8,128)(2,1)} %param.11) | data formatting | bytes 18087936 | tf_op args[1]
  24.2 1.2 slice.104.wt_ref
  25.5 0.0 copy-done.16
  25.5 0.1 broadcast_in_dim.39
  25.5 0.1 reshape_reshape.6.skip_ref
  25.6 14.5 %all-to-all-done = bf16[4,16,15,1024]{3,0,2,1:T(4,128)(2,1)S(1)} async-done(((bf16[4,16,15,1024]{3,0,2,1:T(4,128)(2,1)}), bf16[4,16,15,1024]{3,0,2,1:T(4,128)(2,1)S(1)}, u32[]{:S(2)}, u32[]{:S(2)}) %all-to-all-start) | async-done | bytes 1966112 | tf_op jit(solution)/shard_map/all_to_all | solution.py:407
  40.1 2.2 copy.27
  42.3 3.0 %squeeze.4 = bf16[64,15,1024]{2,0,1:T(8,128)(2,1)S(1)} reshape(bf16[16,4,1,15,1024]{4,1,0,3,2:T(4,128)(2,1)} %copy.27) | data formatting | bytes 3932160 | tf_op jit(solution)/shard_map/squeeze | solution.py:408
  45.3 0.0 copy-done.12
  45.4 20.8 %shard_map.100 = bf16[960,2048]{1,0:T(8,128)(2,1)S(1)} custom-call(bf16[960,1024]{1,0:T(8,128)(2,1)S(1)} %bitcast.51, bf16[1024,4416]{1,0:T(8,128)(2,1)} %copy.29.wx_ref.wz_ref, bf16[1024,320]{1,0:T(8,128)(2,1)S(1)} %slice.104.wt_ref, f32[1,32]{1,0:T(1,128)S(1)} %bitcast.54, f32[1,32]{1,0:T(1,128)S(1)} %bitcast.55, f32[1,2048]{1,0:T(1,128)S(1)} %reshape_reshape.6.skip_ref), custom_call_target="tpu_custom_call" | custom-call | flops 5221908480 | bytes 10813440 | tf_op jit(solution)/shard_map/pallas_call | solution.py:121
  66.1 4.1 %copy.37 = bf16[15,64,2048]{2,0,1:T(8,128)(2,1)} copy(bf16[15,64,2048]{2,1,0:T(8,128)(2,1)S(1)} %bitcast.49) | data formatting | bytes 7864320 | tf_op jit(solution)/shard_map/reshape | solution.py:413
  70.2 4.9 %all-to-all-start.1 = ((bf16[64,1,15,2048]{3,2,1,0:T(8,128)(2,1)}), bf16[64,1,15,2048]{3,2,1,0:T(8,128)(2,1)}, u32[]{:S(2)}, u32[]{:S(2)}) async-start(bf16[64,1,15,2048]{3,2,1,0:T(8,128)(2,1)} %bitcast.58), calls=%async_computation.1 | async-start | bytes 8388608 | tf_op jit(solution)/shard_map/all_to_all | solution.py:414
  75.1 16.6 %shard_map.101 = (bf16[960,2048]{1,0:T(8,128)(2,1)S(1)}, bf16[1024,2048]{1,0:T(8,128)(2,1)S(1)}, bf16[1024,128]{1,0:T(8,128)(2,1)S(1)}, f32[1024,128]{1,0:T(8,128)S(1)}) custom-call(bf16[960,1024]{1,0:T(8,128)(2,1)S(1)} %bitcast.46, bf16[1024,4416]{1,0:T(8,128)(2,1)} %copy.29.wx_ref.wz_ref, bf16[1024,320]{1,0:T(8,128)(2,1)S(1)} %slice.104.wt_ref, ...), custom_call_target="tpu_custom_call" | custom-call | flops 4718592000 | bytes 14745600 | tf_op jit(solution)/shard_map/pallas_call | solution.py:191
  91.8 0.0 copy-start.4
  91.8 1.9 copy-done.4
  93.7 1.9 copy-done.7
  95.6 35.6 %all-to-all-done.1 = bf16[64,1,15,2048]{3,2,1,0:T(8,128)(2,1)} async-done(((bf16[64,1,15,2048]{3,2,1,0:T(8,128)(2,1)}), bf16[64,1,15,2048]{3,2,1,0:T(8,128)(2,1)}, u32[]{:S(2)}, u32[]{:S(2)}) %all-to-all-start.1) | async-done | bytes 3932192 | tf_op jit(solution)/shard_map/all_to_all | solution.py:414
  131.2 5.4 %copy.38 = bf16[16,4,1,15,2048]{4,1,0,3,2:T(4,128)(2,1)S(1)} copy(bf16[16,4,1,15,2048]{4,3,1,0,2:T(8,128)(2,1)} %bitcast.10) | data formatting | bytes 7864320 | tf_op jit(solution)/shard_map/all_to_all | solution.py:414
  136.6 4.2 %copy.32 = bf16[4,16,1,15,2048]{4,3,1,0,2:T(8,128)(2,1)} copy(bf16[4,16,1,15,2048]{4,0,1,3,2:T(4,128)(2,1)S(1)} %bitcast.59) | data formatting | bytes 7864320 | tf_op jit(solution)/shard_map/all_to_all | solution.py:414
  140.7 5.1 %reshape.263.x_ref = bf16[960,2048]{1,0:T(8,128)(2,1)} reshape(bf16[4,16,1,15,2048]{4,3,1,0,2:T(8,128)(2,1)} %copy.32) | data formatting | bytes 7864320 | tf_op jit(solution)/shard_map/reshape | solution.py:414
  145.9 2.1 copy-done
  148.0 5.8 %shard_map.103 = (bf16[1024,2048]{1,0:T(8,128)(2,1)S(1)}, bf16[256,2048]{1,0:T(8,128)(2,1)S(1)}) custom-call(bf16[960,2048]{1,0:T(8,128)(2,1)S(1)} %copy-done, bf16[1024,128]{1,0:T(8,128)(2,1)S(1)} %get-tuple-element.13.small_ref, f32[1024,128]{1,0:T(8,128)S(1)} %get-tuple-element.14.decay_ref), custom_call_target="tpu_custom_call" | custom-call | flops 503316480 | bytes 7864320 | tf_op jit(solution)/shard_map/pallas_call | solution.py:257
  153.8 2.0 copy-done.6
  155.8 1.0 copy-done.10
  156.8 4.8 %all-to-all-start.2 = ((bf16[8,32,2048]{2,1,0:T(8,128)(2,1)}), bf16[8,32,2048]{2,1,0:T(8,128)(2,1)S(1)}, u32[]{:S(2)}, u32[]{:S(2)}) async-start(bf16[8,32,2048]{2,1,0:T(8,128)(2,1)} %bitcast.52), calls=%async_computation.2 | async-start | bytes 2097152 | tf_op jit(solution)/shard_map/all_to_all | solution.py:376
  161.6 32.7 %all-gather.1 = f32[8,4,32]{2,1,0:T(4,128)S(1)} all-gather(f32[1,4,32]{2,1,0:T(4,128)S(1)} %bitcast.62), channel_id=2, replica_groups=mesh['tm'=16,'space'=8] {'space'}, dimensions={0}, use_global_device_ids=true | all-gather | bytes 4608 | tf_op jit(solution)/shard_map/all_gather | solution.py:372
  194.3 0.6 slice_bitcast_fusion
  194.9 0.7 broadcast_in_dim.43
  195.6 0.8 mul.87
  196.4 0.7 broadcast_in_dim.44
  197.0 0.8 broadcast_in_dim.45
  197.8 1.3 broadcast_in_dim.46
  199.1 1.4 broadcast_in_dim.47
  200.5 1.3 broadcast_in_dim.48
  201.8 1.4 broadcast_in_dim.49
  203.2 1.3 broadcast_in_dim.50
  204.5 1.4 broadcast_in_dim.51
  205.9 1.3 broadcast_in_dim.52
  207.1 1.4 broadcast_in_dim.53
  208.5 1.3 broadcast_in_dim.54
  209.8 1.4 broadcast_in_dim.55
  211.2 0.7 broadcast_dynamic-update-slice_fusion
  211.9 0.0 all-to-all-done.2
  211.9 0.7 fusion.7
  212.6 0.7 fusion.6
  213.3 1.4 convert_dynamic-update-slice_fusion.1
  214.7 1.5 fusion.5
  216.2 1.5 convert_dynamic-update-slice_fusion
  217.7 1.4 fusion.4
  219.1 1.4 fusion.8
  220.5 3.8 %all-to-all-start.3 = ((bf16[8,32,2048]{2,1,0:T(8,128)(2,1)}), bf16[8,32,2048]{2,1,0:T(8,128)(2,1)S(1)}, u32[]{:S(2)}, u32[]{:S(2)}) async-start(bf16[8,32,2048]{2,1,0:T(8,128)(2,1)} %fusion.8), calls=%async_computation.3 | async-start | bytes 2097152 | tf_op jit(solution)/shard_map/all_to_all | solution.py:382
  224.3 1.3 broadcast_in_dim.41
  225.6 0.8 reshape_reshape.7.skip_ref
  226.4 2.1 copy-done.1
  228.5 2.2 copy-done.5
  230.7 2.7 %shard_map.102.local_ref = f32[960,2048]{1,0:T(8,128)S(1)} custom-call(bf16[960,2048]{1,0:T(8,128)(2,1)S(1)} %copy-done.1, bf16[1024,2048]{1,0:T(8,128)(2,1)S(1)} %copy-done.5, f32[1,2048]{1,0:T(1,128)S(1)} %reshape_reshape.7.skip_ref), custom_call_target="tpu_custom_call" | custom-call | flops 503316480 | bytes 15728640 | tf_op jit(solution)/shard_map/pallas_call | solution.py:294
  233.5 0.0 copy-start.2
  233.5 3.0 %copy-done.2 = f32[960,2048]{1,0:T(8,128)} copy-done((f32[960,2048]{1,0:T(8,128)}, f32[960,2048]{1,0:T(8,128)S(1)}, u32[]{:S(2)}) %copy-start.2) | copy-done | bytes 7864344
  236.5 0.0 all-to-all-done.3
  236.5 0.9 copy-done.9
  237.5 16.3 %shard_map.104 = bf16[960,1024]{1,0:T(8,128)(2,1)} custom-call(f32[960,2048]{1,0:T(8,128)} %copy-done.2, bf16[960,2048]{1,0:T(8,128)(2,1)} %copy-done.7, bf16[1024,128]{1,0:T(8,128)(2,1)S(1)} %copy-done.9, f32[1024,128]{1,0:T(8,128)S(1)} %get-tuple-element.14.decay_ref, bf16[1024,2048]{1,0:T(8,128)(2,1)} %copy-done.6, bf16[256,2048]{1,0:T(8,128)(2,1)S(1)} %bitcast.48, ...), custom_call_target="tpu_custom_call" | custom-call | flops 4278190080 | bytes 15728640 | tf_op jit(solution)/shard_map/pallas_call | solution.py:343
  (22 shorter events, 0.1 us)
Async XLA Ops:
  4.3 35.8 %all-to-all-start = ((bf16[4,16,15,1024]{3,0,2,1:T(4,128)(2,1)}), bf16[4,16,15,1024]{3,0,2,1:T(4,128)(2,1)S(1)}, u32[]{:S(2)}, u32[]{:S(2)}) async-start(bf16[4,16,15,1024]{3,0,2,1:T(4,128)(2,1)} %bitcast.61), calls=%async_computation | async-start | bytes 3932160 | tf_op jit(solution)/shard_map/all_to_all | solution.py:407
  12.3 13.2 %copy-start.16 = (f32[32]{0:T(128)S(1)}, f32[32]{0:T(128)}, u32[]{:S(2)}) copy-start(f32[32]{0:T(128)} %param.17) | copy-start | bytes 388
  40.1 5.2 %copy-start.12 = (f32[32]{0:T(128)S(1)}, f32[32]{0:T(128)}, u32[]{:S(2)}) copy-start(f32[32]{0:T(128)} %param.15) | copy-start | bytes 388
  40.1 5.2 %copy-start.13 = (f32[32]{0:T(128)S(1)}, f32[32]{0:T(128)}, u32[]{:S(2)}) copy-start(f32[32]{0:T(128)} %param.13) | copy-start | bytes 388
  70.2 4.9 %copy-start.3 = (bf16[4,3,80,1024]{3,2,1,0:T(8,128)(2,1)S(1)}, bf16[4,3,80,1024]{3,2,1,0:T(8,128)(2,1)}, u32[]{:S(2)}) copy-start(bf16[4,3,80,1024]{3,2,1,0:T(8,128)(2,1)} %param.10) | copy-start | bytes 5898244
  70.2 4.9 %copy-start.14 = (f32[32]{0:T(128)S(1)}, f32[32]{0:T(128)}, u32[]{:S(2)}) copy-start(f32[32]{0:T(128)} %param.16) | copy-start | bytes 388
  70.2 4.9 %copy-start.15 = (f32[32]{0:T(128)S(1)}, f32[32]{0:T(128)}, u32[]{:S(2)}) copy-start(f32[32]{0:T(128)} %param.14) | copy-start | bytes 388
  70.2 61.0 %all-to-all-start.1 = ((bf16[64,1,15,2048]{3,2,1,0:T(8,128)(2,1)}), bf16[64,1,15,2048]{3,2,1,0:T(8,128)(2,1)}, u32[]{:S(2)}, u32[]{:S(2)}) async-start(bf16[64,1,15,2048]{3,2,1,0:T(8,128)(2,1)} %bitcast.58), calls=%async_computation.1 | async-start | bytes 8388608 | tf_op jit(solution)/shard_map/all_to_all | solution.py:414
  91.8 1.9 copy-start.4
  93.7 1.9 copy-start.7
  95.6 50.3 %copy-start.8 = (bf16[1024,128]{1,0:T(8,128)(2,1)}, bf16[1024,128]{1,0:T(8,128)(2,1)S(1)}, u32[]{:S(2)}) copy-start(bf16[1024,128]{1,0:T(8,128)(2,1)S(1)} %get-tuple-element.13.small_ref) | copy-start | bytes 786436
  145.9 2.1 copy-start
  153.8 2.0 copy-start.6
  155.8 1.0 copy-start.10
  156.8 55.1 %all-to-all-start.2 = ((bf16[8,32,2048]{2,1,0:T(8,128)(2,1)}), bf16[8,32,2048]{2,1,0:T(8,128)(2,1)S(1)}, u32[]{:S(2)}, u32[]{:S(2)}) async-start(bf16[8,32,2048]{2,1,0:T(8,128)(2,1)} %bitcast.52), calls=%async_computation.2 | async-start | bytes 2097152 | tf_op jit(solution)/shard_map/all_to_all | solution.py:376
  220.5 16.0 %all-to-all-start.3 = ((bf16[8,32,2048]{2,1,0:T(8,128)(2,1)}), bf16[8,32,2048]{2,1,0:T(8,128)(2,1)S(1)}, u32[]{:S(2)}, u32[]{:S(2)}) async-start(bf16[8,32,2048]{2,1,0:T(8,128)(2,1)} %fusion.8), calls=%async_computation.3 | async-start | bytes 2097152 | tf_op jit(solution)/shard_map/all_to_all | solution.py:382
  226.4 2.1 copy-start.1
  228.5 2.2 copy-start.5
  230.7 5.8 %copy-start.11 = (f32[2048]{0:T(1024)S(1)}, f32[2048]{0:T(1024)}, u32[]{:S(2)}) copy-start(f32[2048]{0:T(1024)} %param.19) | copy-start | bytes 24580
  233.5 3.1 %copy-start.2 = (f32[960,2048]{1,0:T(8,128)}, f32[960,2048]{1,0:T(8,128)S(1)}, u32[]{:S(2)}) copy-start(f32[960,2048]{1,0:T(8,128)S(1)} %shard_map.102.local_ref) | copy-start | bytes 23592964
  236.5 1.0 copy-start.9

commit v2 on v1

--- a/solution.py
+++ b/solution.py
@@ -219,168 +219,267 @@
     )(tok, w_in, w_tail, bias, alog)
 
 
-def spread_last(cum, spread):
-    last = jnp.broadcast_to(jnp.exp(cum[CHUNK - 1 : CHUNK, :]), (16, HEADS))
-    return mm(split3(last), spread)[:1]
-
-
-def state_kernel(x_ref, small_ref, decay_ref, starts_ref, end_ref, spread):
-    seq = x_ref.shape[0]
-
-    @pl.when(pl.program_id(0) == 0)
-    def _():
-        spread[...] = head_spread()
-
-    state = jnp.zeros((STATE, DI), F32)
-    count = starts_ref.shape[0] // STATE
-    for k in range(count):
-        size = min(CHUNK, seq - k * CHUNK)
-        starts_ref[pl.ds(k * STATE, STATE), :] = state.astype(BF16)
-        decay = decay_ref[pl.ds(k * CHUNK, CHUNK), :]
-        cum, step = decay[:, :HEADS], decay[:, HEADS : 2 * HEADS]
-        tail = (jnp.exp(cum[CHUNK - 1 :, :] - cum) * step)[:size]
-        tail_wide = mm(split3(tail)[:, : 2 * HEADS], spread[: 2 * HEADS, :])
-        x = x_ref[pl.ds(k * CHUNK, size), :].astype(F32)
-        weighted = (x * tail_wide).astype(BF16)
-        inject = small_ref[pl.ds(k * CHUNK, size), :STATE]
-        added = lax.dot_general(inject, weighted, (((0,), (0,)), ((), ())), preferred_element_type=F32)
-        state = spread_last(cum, spread[...]) * state + added
-    end_ref[...] = state.astype(BF16)
-
-
-def space_states(x, small, decay, frames):
-    total = x.shape[0]
-    seq = total // frames
-    padded = decay.shape[0] // frames
+def widen(values, spread):
+    return mm(split3(values), spread[...])
+
+
+def last_row(values):
+    return jnp.broadcast_to(values[CHUNK - 1 :, :], (16, HEADS))
+
+
+def back_kernel(
+    n,
+    x_hbm,
+    w_hbm,
+    z_hbm,
+    tok_hbm,
+    wo_hbm,
+    small_ref,
+    decay_ref,
+    skip_ref,
+    gain_ref,
+    out_ref,
+    x_v,
+    w_v,
+    z_v,
+    tok_v,
+    wo_v,
+    starts,
+    end,
+    got,
+    leaving,
+    entering,
+    tot_mine,
+    tot_got,
+    growth,
+    running,
+    local,
+    y_v,
+    spread,
+    load_sem,
+    send_sem,
+    recv_sem,
+    tot_send,
+    tot_recv,
+    back_send,
+    back_recv,
+):
+    frames, seq = x_v.shape[0], x_v.shape[1]
+    count = w_v.shape[1] // CHUNK
+    halves = n // frames
+    part = STATE // halves
+    me = lax.axis_index("space")
+
+    def load(kind, f):
+        src, dst = ((x_hbm, x_v), (w_hbm, w_v), (z_hbm, z_v), (tok_hbm, tok_v))[kind]
+        return pltpu.make_async_copy(src.at[f], dst.at[f], load_sem.at[kind, f])
+
+    weight_load = pltpu.make_async_copy(wo_hbm, wo_v, load_sem.at[4, 0])
+    for kind in range(4):
+        for f in range(frames):
+            load(kind, f).start()
+    weight_load.start()
+
+    def remote(src, dst, send, recv, device):
+        return pltpu.make_async_remote_copy(
+            src_ref=src,
+            dst_ref=dst,
+            send_sem=send,
+            recv_sem=recv,
+            device_id={"space": device},
+            device_id_type=pl.DeviceIdType.MESH,
+        )
+
+    def state_copy(g, slot):
+        return remote(end.at[g], got.at[slot], send_sem.at[g], recv_sem.at[slot], g)
+
+    def tot_copy(g, slot):
+        return remote(tot_mine.at[g // halves], tot_got.at[slot], tot_send.at[g], tot_recv.at[slot], g)
+
+    def back_copy(g, slot):
+        return remote(leaving.at[g], entering.at[slot], back_send.at[g], back_recv.at[slot], g)
+
+    barrier = pltpu.get_barrier_semaphore()
+    for step in range(1, n):
+        pl.semaphore_signal(
+            barrier,
+            inc=1,
+            device_id={"space": lax.rem(me + step, n)},
+            device_id_type=pl.DeviceIdType.MESH,
+        )
+    spread[...] = head_spread()
+    pl.semaphore_wait(barrier, n - 1)
+
+    def states(f, carry):
+        load(0, f).wait()
+        state = jnp.zeros((STATE, DI), F32)
+        total = jnp.zeros((16, HEADS), F32)
+        for k in range(count):
+            size = min(CHUNK, seq - k * CHUNK)
+            starts[f, pl.ds(k * STATE, STATE), :] = state.astype(BF16)
+            decay = decay_ref[f, pl.ds(k * CHUNK, CHUNK), :]
+            cum, step = decay[:, :HEADS], decay[:, HEADS : 2 * HEADS]
+            tail = (jnp.exp(cum[CHUNK - 1 :, :] - cum) * step)[:size]
+            weighted = (x_v[f, pl.ds(k * CHUNK, size), :].astype(F32) * widen(tail, spread)).astype(BF16)
+            inject = small_ref[f, pl.ds(k * CHUNK, size), :STATE]
+            added = lax.dot_general(
+                inject, weighted, (((0,), (0,)), ((), ())), preferred_element_type=F32
+            )
+            state = widen(last_row(jnp.exp(cum)), spread)[:1] * state + added
+            total = total + last_row(cum)
+        tot_mine[f] = jnp.concatenate([total[:8], jnp.zeros((8, 128 - HEADS), F32)], axis=1)
+        for half in range(halves):
+            g = halves * f + half
+            end[g] = state[half * part : (half + 1) * part].astype(BF16)
+
+            @pl.when(g != me)
+            def _():
+                state_copy(g, me).start()
+                tot_copy(g, me).start()
+
+            @pl.when(g == me)
+            def _():
+                got[me] = end[me]
+                tot_got[me] = tot_mine[f]
+
+        return carry
+
+    lax.fori_loop(0, frames, states, 0)
+
+    def locals_of(f, carry):
+        load(1, f).wait()
+        for k in range(count):
+            size = min(CHUNK, seq - k * CHUNK)
+            rows = pl.ds(k * CHUNK, size)
+            for j in range(HEADS // 2):
+                lanes = pl.ds(j * 128, 128)
+                x_pair = x_v[f, rows, lanes]
+                padded = x_pair
+                if size < CHUNK:
+                    padded = jnp.concatenate([x_pair, jnp.zeros((CHUNK - size, 128), BF16)], axis=0)
+                mixed = mm(w_v[f, rows, lanes], block_pair(padded))
+                local[f, rows, lanes] = mixed + skip_ref[:, lanes] * x_pair.astype(F32)
+        return carry
+
+    lax.fori_loop(0, frames, locals_of, 0)
+
+    def wait_total(s, carry):
+        @pl.when(s != me)
+        def _():
+            tot_copy(s, s).wait_recv()
+
+        return carry
+
+    lax.fori_loop(0, n, wait_total, 0)
+    totals = jnp.concatenate([tot_got[s] for s in range(n)], axis=0)[:, :HEADS]
+    growth[...] = widen(jnp.exp(totals), spread)
+    running[...] = jnp.zeros_like(running)
+
+    def relay(s, carry):
+        @pl.when(s != me)
+        def _():
+            leaving[s] = running[...].astype(BF16)
+            back_copy(s, me).start()
+            state_copy(s, s).wait_recv()
+
+        @pl.when(s == me)
+        def _():
+            entering[me] = running[...].astype(BF16)
+
+        rate = growth[pl.ds(pl.multiple_of(s * 8, 8), 1), :]
+        running[...] = rate * running[...] + got[s].astype(F32)
+        return carry
+
+    lax.fori_loop(0, n, relay, 0)
+    weight_load.wait()
+
+    def finish(f, carry):
+        load(2, f).wait()
+        load(3, f).wait()
+        for half in range(halves):
+            g = halves * f + half
+
+            @pl.when(g != me)
+            def _():
+                back_copy(g, g).wait_recv()
+
+        arrived = jnp.concatenate([entering[halves * f + half] for half in range(halves)], axis=0)
+        arrived = arrived.astype(F32)
+        offset = jnp.zeros((16, HEADS), F32)
+        for k in range(count):
+            size = min(CHUNK, seq - k * CHUNK)
+            rows = pl.ds(k * CHUNK, size)
+            cum = decay_ref[f, pl.ds(k * CHUNK, CHUNK), :HEADS]
+            reach = widen(jnp.exp(offset), spread)[:1]
+            offset = offset + last_row(cum)
+            state = starts[f, pl.ds(k * STATE, STATE), :].astype(F32) + reach * arrived
+            carried = mm(small_ref[f, rows, STATE:], state.astype(BF16))
+            z = z_v[f, rows, :].astype(F32)
+            y = local[f, rows, :] + widen(jnp.exp(cum[:size]), spread) * carried
+            y = y * (z * (1.0 / (1.0 + jnp.exp(-z))))
+            scale = lax.rsqrt(jnp.mean(y * y, axis=1, keepdims=True) + 1e-5)
+            y_v[rows, :] = (y * scale * gain_ref[...]).astype(BF16)
+        out_ref[f] = (mm(y_v[...], wo_v[...]) + tok_v[f].astype(F32)).astype(BF16)
+        return carry
+
+    lax.fori_loop(0, frames, finish, 0)
+
+    def drain(g, carry):
+        @pl.when(g != me)
+        def _():
+            state_copy(g, me).wait_send()
+            tot_copy(g, me).wait_send()
+            back_copy(g, me).wait_send()
+
+        return carry
+
+    lax.fori_loop(0, n, drain, 0)
+
+
+def back_part(x, weights, z, tok, w_out, small, decay, skip_wide, gain):
+    n = lax.axis_size("space")
+    frames, seq = x.shape[0], x.shape[1]
+    padded = weights.shape[1]
     count = padded // CHUNK
-    row = lambda n, width: pl.BlockSpec((n, width), lambda i: (i, 0))
+    part = frames * STATE // n
+    anywhere = pl.BlockSpec(memory_space=pl.ANY)
+    in_vmem = pl.BlockSpec(memory_space=pltpu.VMEM)
+    dma = pltpu.SemaphoreType.DMA
     return pl.pallas_call(
-        state_kernel,
-        out_shape=(
-            jax.ShapeDtypeStruct((frames * count * STATE, DI), BF16),
-            jax.ShapeDtypeStruct((frames * STATE, DI), BF16),
+        functools.partial(back_kernel, n),
+        out_shape=jax.ShapeDtypeStruct((frames, seq, D), BF16),
+        in_specs=[anywhere] * 5 + [in_vmem] * 4,
+        out_specs=in_vmem,
+        scratch_shapes=[
+            pltpu.VMEM((frames, seq, DI), BF16),
+            pltpu.VMEM((frames, padded, DI), BF16),
+            pltpu.VMEM((frames, seq, DI), BF16),
+            pltpu.VMEM((frames, seq, D), BF16),
+            pltpu.VMEM((DI, D), BF16),
+            pltpu.VMEM((frames, count * STATE, DI), BF16),
+            pltpu.VMEM((n, part, DI), BF16),
+            pltpu.VMEM((n, part, DI), BF16),
+            pltpu.VMEM((n, part, DI), BF16),
+            pltpu.VMEM((n, part, DI), BF16),
+            pltpu.VMEM((frames, 8, 128), F32),
+            pltpu.VMEM((n, 8, 128), F32),
+            pltpu.VMEM((n * 8, DI), F32),
+            pltpu.VMEM((part, DI), F32),
+            pltpu.VMEM((frames, seq, DI), F32),
+            pltpu.VMEM((seq, DI), BF16),
+            pltpu.VMEM((3 * HEADS, DI), BF16),
+            dma((5, frames)),
+            dma((n,)),
+            dma((n,)),
+            dma((n,)),
+            dma((n,)),
+            dma((n,)),
+            dma((n,)),
+        ],
+        compiler_params=pltpu.CompilerParams(
+            collective_id=0, has_side_effects=True, vmem_limit_bytes=56 * MIB
         ),
-        grid=(frames,),
-        in_specs=[row(seq, DI), row(padded, 2 * STATE), row(padded, 128)],
-        out_specs=(row(count * STATE, DI), row(STATE, DI)),
-        scratch_shapes=[pltpu.VMEM((3 * HEADS, DI), BF16)],
-        compiler_params=pltpu.CompilerParams(vmem_limit_bytes=32 * MIB),
-        cost_estimate=pl.CostEstimate(
-            flops=2 * total * 128 * DI, bytes_accessed=4 * total * DI, transcendentals=0
-        ),
-    )(x, small, decay)
-
-
-def local_kernel(x_ref, w_ref, skip_ref, out_ref):
-    seq = x_ref.shape[0]
-    for k in range(w_ref.shape[0] // CHUNK):
-        size = min(CHUNK, seq - k * CHUNK)
-        rows = pl.ds(k * CHUNK, size)
-        for j in range(HEADS // 2):
-            lanes = pl.ds(j * 128, 128)
-            x_pair = x_ref[rows, lanes]
-            padded = x_pair
-            if size < CHUNK:
-                padded = jnp.concatenate([x_pair, jnp.zeros((CHUNK - size, 128), BF16)], axis=0)
-            local = mm(w_ref[rows, lanes], block_pair(padded))
-            out_ref[rows, lanes] = local + skip_ref[:, lanes] * x_pair.astype(F32)
-
-
-def space_local(x, weights, skip_wide, frames):
-    total = x.shape[0]
-    seq = total // frames
-    padded = weights.shape[0] // frames
-    row = lambda n, width: pl.BlockSpec((n, width), lambda i: (i, 0))
-    return pl.pallas_call(
-        local_kernel,
-        out_shape=jax.ShapeDtypeStruct((total, DI), F32),
-        grid=(frames,),
-        in_specs=[
-            row(seq, DI),
-            row(padded, DI),
-            pl.BlockSpec((1, DI), lambda i: (0, 0), pipeline_mode=pl.Buffered(1)),
-        ],
-        out_specs=row(seq, DI),
-        compiler_params=pltpu.CompilerParams(vmem_limit_bytes=32 * MIB),
-        cost_estimate=pl.CostEstimate(
-            flops=2 * total * 128 * DI, bytes_accessed=8 * total * DI, transcendentals=0
-        ),
-    )(x, weights, skip_wide)
-
-
-def finish_kernel(local_ref, z_ref, small_ref, decay_ref, starts_ref, from_ref, gain_ref, wo_ref, tok_ref, out_ref, spread, y_ref):
-    seq = local_ref.shape[0]
-
-    @pl.when(pl.program_id(0) == 0)
-    def _():
-        spread[...] = head_spread()
-
-    offset = jnp.zeros((1, HEADS), F32)
-    entering = from_ref[...].astype(F32)
-    for k in range(decay_ref.shape[0] // CHUNK):
-        size = min(CHUNK, seq - k * CHUNK)
-        rows = pl.ds(k * CHUNK, size)
-        cum = decay_ref[pl.ds(k * CHUNK, CHUNK), :HEADS]
-        reach = mm(split3(jnp.broadcast_to(jnp.exp(offset), (16, HEADS))), spread[...])[:1]
-        offset = offset + cum[CHUNK - 1 :, :]
-        state = (starts_ref[pl.ds(k * STATE, STATE), :].astype(F32) + reach * entering).astype(BF16)
-        carried = mm(small_ref[rows, STATE:], state)
-        grown = mm(split3(jnp.exp(cum[:size])), spread[...])
-        z = z_ref[rows, :].astype(F32)
-        y = (local_ref[rows, :] + grown * carried) * (z * (1.0 / (1.0 + jnp.exp(-z))))
-        scale = lax.rsqrt(jnp.mean(y * y, axis=1, keepdims=True) + 1e-5)
-        y_ref[rows, :] = (y * scale * gain_ref[...]).astype(BF16)
-    out_ref[...] = (mm(y_ref[...], wo_ref[...]) + tok_ref[...].astype(F32)).astype(BF16)
-
-
-def finish(local, z, small, decay, starts, entering, gain, w_out, tok, frames):
-    total = local.shape[0]
-    seq = total // frames
-    padded = decay.shape[0] // frames
-    count = padded // CHUNK
-    whole = lambda shape: pl.BlockSpec(shape, lambda i: (0, 0), pipeline_mode=pl.Buffered(1))
-    row = lambda n, width: pl.BlockSpec((n, width), lambda i: (i, 0))
-    return pl.pallas_call(
-        finish_kernel,
-        out_shape=jax.ShapeDtypeStruct((total, D), BF16),
-        grid=(frames,),
-        in_specs=[
-            row(seq, DI),
-            row(seq, DI),
-            row(padded, 2 * STATE),
-            row(padded, 128),
-            row(count * STATE, DI),
-            row(STATE, DI),
-            whole((1, DI)),
-            whole((DI, D)),
-            row(seq, D),
-        ],
-        out_specs=row(seq, D),
-        scratch_shapes=[pltpu.VMEM((3 * HEADS, DI), BF16), pltpu.VMEM((seq, DI), BF16)],
-        compiler_params=pltpu.CompilerParams(vmem_limit_bytes=48 * MIB),
-        cost_estimate=pl.CostEstimate(
-            flops=2 * total * (D + 64) * DI, bytes_accessed=8 * total * DI, transcendentals=total * DI
-        ),
-    )(local, z, small, decay, starts, entering, gain, w_out, tok)
-
-
-def space_exchange(end, totals):
-    n = lax.axis_size("space")
-    frames = totals.shape[0]
-    part = end.shape[0] // n
-    per_frame = STATE // part
-    growth = jnp.exp(lax.all_gather(totals, "space"))
-    mine = lax.axis_index("space") // per_frame
-    growth = lax.dynamic_index_in_dim(growth, mine, axis=1, keepdims=False)
-    growth = jnp.repeat(growth, HEAD_DIM, axis=1)[:, None, :]
-    got = lax.all_to_all(end.reshape(n, part, DI), "space", 0, 0, tiled=True)
-    running = jnp.zeros((part, DI), F32)
-    starts = []
-    for device in range(n):
-        starts.append(running.astype(BF16))
-        running = growth[device] * running + got[device].astype(F32)
-    back = lax.all_to_all(jnp.stack(starts), "space", 0, 0, tiled=True)
-    return back.reshape(frames * STATE, DI)
+    )(x, weights, z, tok, w_out, small, decay, skip_wide, gain)
 
 
 def body(
@@ -413,11 +512,18 @@
     returned = jnp.swapaxes(time_out.reshape(items, n_tm * frames, DI), 0, 1)[:, None]
     time_out = lax.all_to_all(returned, "tm", 0, 1, tiled=True).reshape(-1, DI)
 
-    totals = decay.reshape(frames, -1, CHUNK, 128)[:, :, CHUNK - 1, :HEADS].sum(axis=1)
-    starts, end = space_states(time_out, small, decay, frames)
-    entering = space_exchange(end, totals)
-    local = space_local(time_out, weights, wide(skip_space), frames)
-    out = finish(local, gate, small, decay, starts, entering, one(norm_gain), w_out, flat, frames)
+    framed = lambda v: v.reshape(frames, -1, v.shape[-1])
+    out = back_part(
+        framed(time_out),
+        framed(weights),
+        framed(gate),
+        framed(flat),
+        w_out,
+        framed(small),
+        framed(decay),
+        wide(skip_space),
+        one(norm_gain),
+    )
     return out.reshape(tokens.shape)
 
 

time: 257 us -> 195 us (0.76)
  the two profiles are of different devices: /device:TPU:0 before, /device:TPU:54 now
where the time goes in v2:
time: 195 us; the launch traced here: 194 us
  Pallas kernels  88.1 us (45%)
  local copies, waits for them, and re-layouts  47.7 us (24%)
  waiting for transfers between devices  44.6 us (23%)
  starting transfers between devices  13.8 us (7%)
    pallas_call x1, Pallas kernels, back_part(): pl.pallas_call(functools.partial(back_kernel, n), out_shape=jax.ShapeDtyp...  50.7 us
    all_to_all x1, waiting for transfers between devices, body(): time_out = lax.all_to_all(returned, 'tm', 0, 1, tiled=True).reshape(-1, DI)  32.3 us
    unnamed x25, local copies, waits for them, and re-layouts  24.8 us
    pallas_call x1, Pallas kernels, time_scan(): pl.pallas_call(time_kernel, out_shape=jax.ShapeDtypeStruct((total, DI), B...  20.7 us
    pallas_call x1, Pallas kernels, home_part(): pl.pallas_call(home_kernel, out_shape=(jax.ShapeDtypeStruct((total, DI),...  16.7 us
    all_to_all x1, waiting for transfers between devices, body(): lax.all_to_all(tokens.reshape(frames, n_tm, items, D), 'tm', 1, 0, tiled=...  12.3 us
    all_to_all x2, local copies, waits for them, and re-layouts, body(): time_out = lax.all_to_all(returned, 'tm', 0, 1, tiled=True).reshape(-1, DI)  7.46 us
    all_to_all x1, starting transfers between devices, body(): lax.all_to_all(tokens.reshape(frames, n_tm, items, D), 'tm', 1, 0, tiled=...  7.23 us
  transfers between devices with their start and end apart: 2, of which 2 were waited for; matrix products, arithmetic and copies ran while one was open for 7% of the time, Pallas kernels for 9%

profile of v2, /device:TPU:54, one launch (start us, length us, event | category | flops | bytes accessed | tf_op | source)
XLA Modules:
  0.0 194.4 jit_solution(9251961986275768216)
XLA Ops:
  0.0 4.3 %copy.28 = bf16[4,3,80,1024]{3,0,2,1:T(4,128)(2,1)} copy(bf16[4,3,80,1024]{3,2,1,0:T(8,128)(2,1)} %param.10) | data formatting | bytes 3932160 | tf_op args[0]
  4.3 7.2 %all-to-all-start = ((bf16[4,16,15,1024]{3,0,2,1:T(4,128)(2,1)}), bf16[4,16,15,1024]{3,0,2,1:T(4,128)(2,1)S(1)}, u32[]{:S(2)}, u32[]{:S(2)}) async-start(bf16[4,16,15,1024]{3,0,2,1:T(4,128)(2,1)} %bitcast.48), calls=%async_computation | async-start | bytes 3932160 | tf_op jit(solution)/shard_map/all_to_all | solution.py:506
  11.6 0.0 copy-start.9
  11.6 12.2 %copy.31.wx_ref.wz_ref = bf16[1024,4416]{1,0:T(8,128)(2,1)} copy(bf16[1024,4416]{0,1:T(8,128)(2,1)} %param.11) | data formatting | bytes 18087936 | tf_op args[1]
  23.7 1.2 slice.4.wt_ref
  24.9 0.0 copy-done.9
  25.0 0.1 broadcast_in_dim.9
  25.0 0.1 reshape_reshape.12.skip_ref
  25.1 12.3 %all-to-all-done = bf16[4,16,15,1024]{3,0,2,1:T(4,128)(2,1)S(1)} async-done(((bf16[4,16,15,1024]{3,0,2,1:T(4,128)(2,1)}), bf16[4,16,15,1024]{3,0,2,1:T(4,128)(2,1)S(1)}, u32[]{:S(2)}, u32[]{:S(2)}) %all-to-all-start) | async-done | bytes 1966112 | tf_op jit(solution)/shard_map/all_to_all | solution.py:506
  37.4 0.0 copy-start.5
  37.4 0.0 copy-start.6
  37.4 2.2 %copy.29 = bf16[16,4,1,15,1024]{4,1,0,3,2:T(4,128)(2,1)} copy(bf16[16,4,1,15,1024]{4,1,3,0,2:T(4,128)(2,1)S(1)} %bitcast.47) | data formatting | bytes 3932160 | tf_op jit(solution)/shard_map/all_to_all | solution.py:506
  39.6 3.0 %squeeze.3 = bf16[64,15,1024]{2,0,1:T(8,128)(2,1)S(1)} reshape(bf16[16,4,1,15,1024]{4,1,0,3,2:T(4,128)(2,1)} %copy.29) | data formatting | bytes 3932160 | tf_op jit(solution)/shard_map/squeeze | solution.py:507
  42.6 0.0 copy-done.5
  42.7 0.0 copy-done.6
  42.7 20.7 %shard_map.100 = bf16[960,2048]{1,0:T(8,128)(2,1)S(1)} custom-call(bf16[960,1024]{1,0:T(8,128)(2,1)S(1)} %bitcast.37, bf16[1024,4416]{1,0:T(8,128)(2,1)} %copy.31.wx_ref.wz_ref, bf16[1024,320]{1,0:T(8,128)(2,1)S(1)} %slice.4.wt_ref, f32[1,32]{1,0:T(1,128)S(1)} %bitcast.40, f32[1,32]{1,0:T(1,128)S(1)} %bitcast.41, f32[1,2048]{1,0:T(1,128)S(1)} %reshape_reshape.12.skip_ref), custom_call_target="tpu_custom_call" | custom-call | flops 5221908480 | bytes 10813440 | tf_op jit(solution)/shard_map/pallas_call | solution.py:121
  63.4 4.1 %copy.40 = bf16[15,64,2048]{2,0,1:T(8,128)(2,1)} copy(bf16[15,64,2048]{2,1,0:T(8,128)(2,1)S(1)} %bitcast.36) | data formatting | bytes 7864320 | tf_op jit(solution)/shard_map/reshape | solution.py:512
  67.5 0.0 copy-start.10
  67.5 0.0 copy-start
  67.5 0.0 copy-start.7
  67.5 0.0 copy-start.8
  67.5 6.6 %all-to-all-start.1 = ((bf16[64,1,15,2048]{3,2,1,0:T(8,128)(2,1)}), bf16[64,1,15,2048]{3,2,1,0:T(8,128)(2,1)}, u32[]{:S(2)}, u32[]{:S(2)}) async-start(bf16[64,1,15,2048]{3,2,1,0:T(8,128)(2,1)} %bitcast.44), calls=%async_computation.1 | async-start | bytes 8388608 | tf_op jit(solution)/shard_map/all_to_all | solution.py:513
  74.1 0.0 copy-done.10
  74.1 0.1 broadcast_in_dim.11
  74.2 0.7 reshape_reshape.15.skip_ref
  74.8 0.0 copy-done
  74.8 0.0 copy-done.7
  74.8 0.0 copy-done.8
  74.8 16.7 %shard_map.101 = (bf16[960,2048]{1,0:T(8,128)(2,1)S(1)}, bf16[1024,2048]{1,0:T(8,128)(2,1)S(1)}, bf16[1024,128]{1,0:T(8,128)(2,1)S(1)}, f32[1024,128]{1,0:T(8,128)S(1)}) custom-call(bf16[960,1024]{1,0:T(8,128)(2,1)S(1)} %bitcast.33, bf16[1024,4416]{1,0:T(8,128)(2,1)} %copy.31.wx_ref.wz_ref, bf16[1024,320]{1,0:T(8,128)(2,1)S(1)} %slice.4.wt_ref, ...), custom_call_target="tpu_custom_call" | custom-call | flops 4718592000 | bytes 14745600 | tf_op jit(solution)/shard_map/pallas_call | solution.py:191
  91.5 0.0 copy-start.1
  91.5 1.9 %copy-done.1 = bf16[1024,2048]{1,0:T(8,128)(2,1)} copy-done((bf16[1024,2048]{1,0:T(8,128)(2,1)}, bf16[1024,2048]{1,0:T(8,128)(2,1)S(1)}, u32[]{:S(2)}) %copy-start.1) | copy-done | bytes 4194328
  93.5 0.0 copy-start.2
  93.5 1.9 copy-done.2
  95.3 0.0 copy-start.3
  95.4 0.8 copy-done.3
  96.1 0.0 copy-start.4
  96.1 0.7 copy-done.4
  96.9 32.3 %all-to-all-done.1 = bf16[64,1,15,2048]{3,2,1,0:T(8,128)(2,1)} async-done(((bf16[64,1,15,2048]{3,2,1,0:T(8,128)(2,1)}), bf16[64,1,15,2048]{3,2,1,0:T(8,128)(2,1)}, u32[]{:S(2)}, u32[]{:S(2)}) %all-to-all-start.1) | async-done | bytes 3932192 | tf_op jit(solution)/shard_map/all_to_all | solution.py:513
  129.1 5.4 %copy.41 = bf16[16,4,1,15,2048]{4,1,0,3,2:T(4,128)(2,1)S(1)} copy(bf16[16,4,1,15,2048]{4,3,1,0,2:T(8,128)(2,1)} %bitcast.10) | data formatting | bytes 7864320 | tf_op jit(solution)/shard_map/all_to_all | solution.py:513
  134.5 2.1 %copy.34 = bf16[4,16,1,15,2048]{4,0,3,1,2:T(4,128)(2,1)S(1)} copy(bf16[4,16,1,15,2048]{4,0,1,3,2:T(4,128)(2,1)S(1)} %bitcast.45) | data formatting | bytes 7864320 | tf_op jit(solution)/shard_map/all_to_all | solution.py:513
  136.6 4.1 %copy.36.x_hbm = bf16[4,240,2048]{2,1,0:T(8,128)(2,1)} copy(bf16[4,240,2048]{2,0,1:T(4,128)(2,1)S(1)} %bitcast.46) | data formatting | bytes 7864320 | tf_op jit(solution)/shard_map/reshape;reshape | solution.py:515
  140.7 50.7 %shard_map.102 = bf16[4,240,1024]{2,1,0:T(8,128)(2,1)} custom-call(bf16[4,240,2048]{2,1,0:T(8,128)(2,1)} %copy.36.x_hbm, bf16[4,256,2048]{2,1,0:T(8,128)(2,1)} %bitcast.34, bf16[4,240,2048]{2,1,0:T(8,128)(2,1)} %bitcast.35, bf16[4,240,1024]{2,1,0:T(8,128)(2,1)} %bitcast.32, bf16[2048,1024]{1,0:T(8,128)(2,1)} %wo_hbm.1, bf16[4,256,128]{2,1,0:T(8,128)(2,1)} %bitcast.39, ...), custom_call_target="tpu_custom_call" | custom-call | tf_op jit(solution)/shard_map/pallas_call | solution.py:448
  191.4 3.0 %copy.43 = bf16[4,3,80,1024]{3,2,1,0:T(8,128)(2,1)} copy(bf16[4,3,80,1024]{3,2,1,0:T(8,128)(2,1)} %bitcast.49) | data formatting | bytes 3932160
Async XLA Ops:
  4.3 33.1 %all-to-all-start = ((bf16[4,16,15,1024]{3,0,2,1:T(4,128)(2,1)}), bf16[4,16,15,1024]{3,0,2,1:T(4,128)(2,1)S(1)}, u32[]{:S(2)}, u32[]{:S(2)}) async-start(bf16[4,16,15,1024]{3,0,2,1:T(4,128)(2,1)} %bitcast.48), calls=%async_computation | async-start | bytes 3932160 | tf_op jit(solution)/shard_map/all_to_all | solution.py:506
  11.6 13.4 %copy-start.9 = (f32[32]{0:T(128)S(1)}, f32[32]{0:T(128)}, u32[]{:S(2)}) copy-start(f32[32]{0:T(128)} %param.17) | copy-start | bytes 388
  37.4 5.2 %copy-start.5 = (f32[32]{0:T(128)S(1)}, f32[32]{0:T(128)}, u32[]{:S(2)}) copy-start(f32[32]{0:T(128)} %param.15) | copy-start | bytes 388
  37.4 5.2 %copy-start.6 = (f32[32]{0:T(128)S(1)}, f32[32]{0:T(128)}, u32[]{:S(2)}) copy-start(f32[32]{0:T(128)} %param.13) | copy-start | bytes 388
  67.5 6.6 %copy-start.10 = (f32[32]{0:T(128)S(1)}, f32[32]{0:T(128)}, u32[]{:S(2)}) copy-start(f32[32]{0:T(128)} %param.18) | copy-start | bytes 388
  67.5 7.3 %copy-start = (bf16[4,3,80,1024]{3,2,1,0:T(8,128)(2,1)S(1)}, bf16[4,3,80,1024]{3,2,1,0:T(8,128)(2,1)}, u32[]{:S(2)}) copy-start(bf16[4,3,80,1024]{3,2,1,0:T(8,128)(2,1)} %param.10) | copy-start | bytes 5898244
  67.5 7.3 %copy-start.7 = (f32[32]{0:T(128)S(1)}, f32[32]{0:T(128)}, u32[]{:S(2)}) copy-start(f32[32]{0:T(128)} %param.16) | copy-start | bytes 388
  67.5 7.3 %copy-start.8 = (f32[32]{0:T(128)S(1)}, f32[32]{0:T(128)}, u32[]{:S(2)}) copy-start(f32[32]{0:T(128)} %param.14) | copy-start | bytes 388
  67.5 61.6 %all-to-all-start.1 = ((bf16[64,1,15,2048]{3,2,1,0:T(8,128)(2,1)}), bf16[64,1,15,2048]{3,2,1,0:T(8,128)(2,1)}, u32[]{:S(2)}, u32[]{:S(2)}) async-start(bf16[64,1,15,2048]{3,2,1,0:T(8,128)(2,1)} %bitcast.44), calls=%async_computation.1 | async-start | bytes 8388608 | tf_op jit(solution)/shard_map/all_to_all | solution.py:513
  91.5 2.0 %copy-start.1 = (bf16[1024,2048]{1,0:T(8,128)(2,1)}, bf16[1024,2048]{1,0:T(8,128)(2,1)S(1)}, u32[]{:S(2)}) copy-start(bf16[1024,2048]{1,0:T(8,128)(2,1)S(1)} %get-tuple-element.9) | copy-start | bytes 12582916
  93.5 1.9 copy-start.2
  95.3 0.8 copy-start.3
  96.1 0.7 copy-start.4

commit v3 on v0

v3 whole, which is shorter than its diff:
```python
import functools

import jax
import jax.numpy as jnp
from jax import lax
from jax.experimental import pallas as pl
from jax.experimental.pallas import tpu as pltpu
from jax.sharding import PartitionSpec as P

D = 1024
HEADS = 32
HEAD_DIM = 64
STATE = 64
DI = 2048
CHUNK = 64
F32 = jnp.float32
BF16 = jnp.bfloat16
MIB = 1 << 20


def mm(a, b):
    return jnp.dot(a, b, preferred_element_type=F32)


def softplus(v):
    return jnp.maximum(v, 0.0) + jnp.log1p(jnp.exp(-jnp.abs(v)))


def split3(v):
    hi = v.astype(BF16)
    rest = v - hi.astype(F32)
    mid = rest.astype(BF16)
    low = (rest - mid.astype(F32)).astype(BF16)
    return jnp.concatenate([hi, mid, low], axis=1)


def head_spread():
    row = lax.broadcasted_iota(jnp.int32, (3 * HEADS, DI), 0) % HEADS
    col = lax.broadcasted_iota(jnp.int32, (3 * HEADS, DI), 1) // HEAD_DIM
    return (row == col).astype(BF16)


def causal_ones():
    row = lax.broadcasted_iota(jnp.int32, (CHUNK, CHUNK), 0)
    col = lax.broadcasted_iota(jnp.int32, (CHUNK, CHUNK), 1)
    return row >= col


def chunk_cumsum(log_decay):
    tri = causal_ones().astype(F32).astype(BF16)
    wide = mm(tri, split3(log_decay))
    return wide[:, :HEADS] + wide[:, HEADS : 2 * HEADS] + wide[:, 2 * HEADS :]


def row_forms(cum, step):
    pair = jnp.concatenate([cum, step, jnp.zeros((CHUNK, 2 * HEADS), F32)], axis=1)
    return jnp.concatenate([pair, pair], axis=0).T


def pair_rows(turned_ref, base, j, lane_low):
    even = turned_ref[pl.ds(base + 2 * j, 1), :]
    odd = turned_ref[pl.ds(base + 2 * j + 1, 1), :]
    return jnp.where(lane_low, even, odd)


def decay_weights(cum_wide, turned_ref, scores2, j, lane_low):
    cum_row = pair_rows(turned_ref, 0, j, lane_low)
    step_row = pair_rows(turned_ref, HEADS, j, lane_low)
    span = jnp.exp(jnp.minimum(cum_wide - cum_row, 0.0))
    return (span * (scores2 * step_row)).astype(BF16)


def masked_scores(readout, inject):
    scores = lax.dot_general(readout, inject, (((1,), (1,)), ((), ())), preferred_element_type=F32)
    scores = jnp.where(causal_ones(), scores, 0.0)
    return jnp.concatenate([scores, scores], axis=1)


def block_pair(x_pair):
    low = lax.broadcasted_iota(jnp.int32, x_pair.shape, 1) < HEAD_DIM
    zero = jnp.zeros_like(x_pair)
    return jnp.concatenate([jnp.where(low, x_pair, zero), jnp.where(low, zero, x_pair)], axis=0)


ITEMS = 16
GROUP = 256
PAIRS = GROUP // 128
TOGETHER = 4
LAG = 1


def nt(a, b):
    return lax.dot_general(a, b, (((1,), (1,)), ((), ())), preferred_element_type=F32)


def tn(a, b):
    return lax.dot_general(a, b, (((0,), (0,)), ((), ())), preferred_element_type=F32)


def rounded(v):
    return v.astype(BF16).astype(F32)


def widen(values, spread):
    return mm(split3(values), spread[...])


def last_row(values):
    return jnp.broadcast_to(values[CHUNK - 1 :, :], (8, HEADS))


def block_kernel(
    n,
    n_space,
    tok_hbm,
    w_hbm,
    wo_hbm,
    bias_t_ref,
    alog_t_ref,
    skip_t_ref,
    bias_s_ref,
    alog_s_ref,
    skip_s_ref,
    gain_ref,
    out_ref,
    tok_v,
    tok_got,
    wz,
    wx,
    wt,
    z_v,
    w_v,
    x_group,
    cum_group,
    out_group,
    leaving,
    small_t,
    turned_t,
    turned_s,
    scores_t,
    cum3,
    cum_s,
    spread,
    skips,
    small_s,
    tail_s,
    grown_s,
    rate_s,
    reach_s,
    x_home,
    tot_mine,
    tot_got,
    growth,
    starts,
    end,
    got,
    going,
    entering,
    y_v,
    square,
    acc,
    load_sem,
    tok_send,
    tok_recv,
    ret_send,
    ret_recv,
    tot_send,
    tot_recv,
    st_send,
    st_recv,
    back_send,
    back_recv,
):
    frames, seq = tok_v.shape[0], tok_v.shape[1]
    padded = w_v.shape[1]
    count = padded // CHUNK
    holders = seq // ITEMS
    total = n * frames
    groups = DI // GROUP
    halves = n_space // frames
    part = STATE // halves
    me = lax.axis_index("tm")
    here = lax.axis_index("space")

    tok_load = pltpu.make_async_copy(tok_hbm, tok_v, load_sem.at[0])
    wz_load = pltpu.make_async_copy(w_hbm.at[pl.ds(0, DI)], wz, load_sem.at[1])
    wt_load = pltpu.make_async_copy(w_hbm.at[pl.ds(2 * DI, wt.shape[0])], wt, load_sem.at[2])
    wx_load = pltpu.make_async_copy(w_hbm.at[pl.ds(DI, DI)], wx, load_sem.at[3])
    wo_load = pltpu.make_async_copy(wo_hbm, wz, load_sem.at[4])
    tok_load.start()
    wt_load.start()
    wz_load.start()
    wx_load.start()

    def remote(src, dst, send, recv, axis, device):
        return pltpu.make_async_remote_copy(
            src_ref=src,
            dst_ref=dst,
            send_sem=send,
            recv_sem=recv,
            device_id={axis: device},
            device_id_type=pl.DeviceIdType.MESH,
        )

    def positions(d):
        return pl.ds(pl.multiple_of(d * ITEMS, ITEMS), ITEMS)

    def frame_rows(d):
        return pl.ds(d * frames, frames)

    def channels(g):
        return pl.ds(pl.multiple_of(g * GROUP, GROUP), GROUP)

    def pair_lanes(j):
        return pl.ds(pl.multiple_of(j * 128, 128), 128)

    def tok_copy(d, source):
        return remote(
            tok_hbm.at[:, positions(d), :],
            tok_got.at[frame_rows(source)],
            tok_send,
            tok_recv,
            "tm",
            d,
        )

    def ret_copy(d, source, g):
        return remote(
            leaving.at[g, frame_rows(d)],
            x_home.at[:, positions(source), channels(g)],
            ret_send,
            ret_recv.at[g],
            "tm",
            d,
        )

    def own_copy(g):
        return pltpu.make_async_copy(
            leaving.at[g, frame_rows(me)], x_home.at[:, positions(me), channels(g)], ret_recv.at[g]
        )

    own_tok = pltpu.make_async_copy(
        tok_hbm.at[:, positions(lax.rem(me, holders)), :], tok_got.at[frame_rows(me)], tok_recv
    )

    def tot_copy(s, slot):
        return remote(
            tot_mine.at[s // halves], tot_got.at[slot], tot_send, tot_recv, "space", s
        )

    def state_copy(s, slot, g):
        return remote(
            end.at[g, s], got.at[g, slot], st_send, st_recv.at[g], "space", s
        )

    def back_copy(s, slot, g):
        return remote(
            going.at[g, s], entering.at[g, slot], back_send, back_recv.at[g], "space", s
        )

    def wait_bytes(ref, sem):
        pltpu.make_async_copy(ref, ref, sem).wait()

    others = pl.ds(0, n_space - 1)
    barrier = pltpu.get_barrier_semaphore()
    for step in range(1, n):
        pl.semaphore_signal(
            barrier,
            inc=1,
            device_id={"tm": lax.rem(me + step, n)},
            device_id_type=pl.DeviceIdType.MESH,
        )
    for step in range(1, n_space):
        pl.semaphore_signal(
            barrier,
            inc=1,
            device_id={"space": lax.rem(here + step, n_space)},
            device_id_type=pl.DeviceIdType.MESH,
        )
    pl.semaphore_wait(barrier, n + n_space - 2)

    def send_tokens(step, carry):
        d = lax.rem(me + step, n)

        @pl.when(d < holders)
        def _():
            tok_copy(d, me).start()

        return carry

    lax.fori_loop(1, n, send_tokens, 0)

    @pl.when(me < holders)
    def _():
        own_tok.start()

    spread[...] = head_spread()
    skips[...] = widen(
        jnp.concatenate(
            [
                jnp.broadcast_to(skip_t_ref[...], (8, HEADS)),
                jnp.broadcast_to(skip_s_ref[...], (8, HEADS)),
            ],
            axis=0,
        ),
        spread,
    )
    square[...] = jnp.zeros_like(square)
    acc[...] = jnp.zeros_like(acc)
    lane_low = lax.broadcasted_iota(jnp.int32, (1, 2 * CHUNK), 1) < CHUNK
    tok_load.wait()
    wt_load.wait()
    wz_load.wait()

    def home(f, carry):
        tok = tok_v[f]
        z_v[f] = nt(tok, wz[...]).astype(BF16)
        tail = nt(tok, wt[...])
        inject = tail[:, 2 * STATE : 3 * STATE].astype(BF16)
        readout = tail[:, 3 * STATE : 4 * STATE].astype(BF16)
        step = softplus(tail[:, 4 * STATE + HEADS : 4 * STATE + 2 * HEADS] + bias_s_ref[...])
        pad = padded - seq
        inject = jnp.concatenate([inject, jnp.zeros((pad, STATE), BF16)], axis=0)
        readout = jnp.concatenate([readout, jnp.zeros((pad, STATE), BF16)], axis=0)
        step = jnp.concatenate([step, jnp.zeros((pad, HEADS), F32)], axis=0)
        small_s[f] = jnp.concatenate([inject, readout], axis=1)
        log_decay = -jnp.exp(alog_s_ref[...]) * step
        offset = jnp.zeros((8, HEADS), F32)
        for k in range(count):
            rows = pl.ds(k * CHUNK, CHUNK)
            part_k = slice(k * CHUNK, (k + 1) * CHUNK)
            cum = chunk_cumsum(log_decay[part_k])
            tail_k = jnp.exp(cum[CHUNK - 1 :, :] - cum) * step[part_k]
            tail_s[f, rows, :] = split3(tail_k)[:, : 2 * HEADS]
            grown_s[f, rows, :] = split3(jnp.exp(cum))
            both = widen(jnp.concatenate([jnp.exp(last_row(cum)), jnp.exp(offset)], axis=0), spread)
            rate_s[f, pl.ds(8 * k, 8), :] = both[:8]
            reach_s[f, pl.ds(8 * k, 8), :] = both[8:]
            offset = offset + last_row(cum)
            turned_s[k] = row_forms(cum, step[part_k])
            cum_s[...] = mm(split3(cum), spread[...])
            scores2 = masked_scores(readout[part_k], inject[part_k])
            for j in range(HEADS // 2):
                lanes = pl.ds(j * 128, 128)
                w_v[f, rows, lanes] = decay_weights(cum_s[:, lanes], turned_s.at[k], scores2, j, lane_low)
        tot_mine[f] = jnp.concatenate([offset, jnp.zeros((8, 128 - HEADS), F32)], axis=1)
        for half in range(halves):
            s = halves * f + half

            @pl.when(s != here)
            def _():
                tot_copy(s, here).start()

            @pl.when(s == here)
            def _():
                tot_got[here] = tot_mine[f]

        return carry

    lax.fori_loop(0, frames, home, 0)
    wo_load.start()
    wx_load.wait()

    @pl.when(me < holders)
    def _():
        wait_bytes(tok_got, tok_recv)
        tail = rounded(nt(tok_got[...].reshape(total * ITEMS, D), wt[...]))
        small_t[0] = tail[:, : 2 * STATE]
        small_t[1] = jnp.concatenate(
            [tail[:, 4 * STATE :], jnp.zeros((total * ITEMS, 128 - 2 * HEADS), F32)], axis=1
        )
        rate = -jnp.exp(alog_t_ref[...])

        def prepare(q, carry):
            several = [q * TOGETHER + u for u in range(TOGETHER)]
            rows = [pl.ds(p, CHUNK, stride=ITEMS) for p in several]
            pairs = [small_t[0, r, :].astype(BF16) for r in rows]
            steps = [softplus(small_t[1, r, :][:, :HEADS] + bias_t_ref[...]) for r in rows]
            scores = [masked_scores(pair[:, STATE:], pair[:, :STATE]) for pair in pairs]
            cums = [chunk_cumsum(rate * step) for step in steps]
            forms = [row_forms(cum, step) for cum, step in zip(cums, steps)]
            for u, p in enumerate(several):
                scores_t[p] = scores[u]
                turned_t[p] = forms[u]
                cum3[p] = split3(cums[u])
            return carry

        lax.fori_loop(0, ITEMS // TOGETHER, prepare, 0)

    wait_bytes(tot_got.at[others], tot_recv)
    totals = jnp.concatenate([tot_got[s] for s in range(n_space)], axis=0)[:, :HEADS]
    growth[...] = widen(jnp.exp(totals), spread)
    wo_load.wait()

    def scan_group(g):
        x = rounded(nt(tok_got[...].reshape(total * ITEMS, D), wx[channels(g), :]))
        cum = mm(cum3[...].reshape(ITEMS * CHUNK, 3 * HEADS), spread[:, channels(g)])
        for jj in range(PAIRS):
            x_group[jj] = x[:, jj * 128 : (jj + 1) * 128]
            cum_group[jj] = cum[:, jj * 128 : (jj + 1) * 128]

        def item(q, inner):
            work = [(q * TOGETHER + u, jj) for u in range(TOGETHER) for jj in range(PAIRS)]
            weights = [
                decay_weights(
                    cum_group[jj, pl.ds(pl.multiple_of(p * CHUNK, CHUNK), CHUNK), :],
                    turned_t.at[p],
                    scores_t[p],
                    g * PAIRS + jj,
                    lane_low,
                )
                for p, jj in work
            ]
            inputs = [x_group[jj, pl.ds(p, CHUNK, stride=ITEMS), :] for p, jj in work]
            mixed = [mm(w, block_pair(x.astype(BF16))) for w, x in zip(weights, inputs)]
            for u, (p, jj) in enumerate(work):
                skip = skips[pl.ds(0, 1), pair_lanes(g * PAIRS + jj)]
                out_group[jj, pl.ds(p, CHUNK, stride=ITEMS), :] = mixed[u] + skip * inputs[u]
            return inner

        lax.fori_loop(0, ITEMS // TOGETHER, item, 0)
        for jj in range(PAIRS):
            leaving[g, :, :, pl.ds(jj * 128, 128)] = (
                out_group[jj].astype(BF16).reshape(total, ITEMS, 128)
            )

        def send(step, inner):
            ret_copy(lax.rem(me + step, n), me, g).start()
            return inner

        lax.fori_loop(1, n, send, 0)
        own_copy(g).start()

    def states(g):
        wait_bytes(x_home.at[:, :, channels(g)], ret_recv.at[g])
        pieces = [(f, k, min(CHUNK, seq - k * CHUNK)) for f in range(frames) for k in range(count)]
        added = []
        for f, k, size in pieces:
            rows = pl.ds(k * CHUNK, size)
            tail_wide = mm(tail_s[f, rows, :], spread[: 2 * HEADS, channels(g)])
            weighted = (x_home[f, rows, channels(g)].astype(F32) * tail_wide).astype(BF16)
            added.append(tn(small_s[f, rows, :STATE], weighted))
        for f in range(frames):
            state = jnp.zeros((STATE, GROUP), F32)
            for k in range(count):
                starts[f, pl.ds(k * STATE, STATE), channels(g)] = state.astype(BF16)
                state = rate_s[f, pl.ds(8 * k, 1), channels(g)] * state + added[f * count + k]
            for half in range(halves):
                end[g, halves * f + half] = state[half * part : (half + 1) * part].astype(BF16)

        def send_state(step, carry):
            state_copy(lax.rem(here + step, n_space), here, g).start()
            return carry

        lax.fori_loop(1, n_space, send_state, 0)
        got[g, here] = end[g, here]

    def relay(g):
        wait_bytes(got.at[g, others], st_recv.at[g])
        running = jnp.zeros((part, GROUP), F32)
        for s in range(n_space):
            going[g, s] = running.astype(BF16)
            running = growth[pl.ds(8 * s, 1), channels(g)] * running + got[g, s].astype(F32)

        def send_back(step, carry):
            back_copy(lax.rem(here + step, n_space), here, g).start()
            return carry

        lax.fori_loop(1, n_space, send_back, 0)
        entering[g, here] = going[g, here]

    def finish(g):
        wait_bytes(entering.at[g, others], back_recv.at[g])

        def frame(f, carry):
            arrived = jnp.concatenate(
                [entering[g, halves * f + half] for half in range(halves)], axis=0
            ).astype(F32)
            sizes = [min(CHUNK, seq - k * CHUNK) for k in range(count)]
            carried, mixed = [], []
            for k, size in enumerate(sizes):
                rows = pl.ds(k * CHUNK, size)
                reach = reach_s[f, pl.ds(8 * k, 1), channels(g)]
                state = starts[f, pl.ds(k * STATE, STATE), channels(g)].astype(F32) + reach * arrived
                product = mm(small_s[f, rows, STATE:], state.astype(BF16))
                carried.append(product * mm(grown_s[f, rows, :], spread[:, channels(g)]))
                for jj in range(PAIRS):
                    lanes = pair_lanes(g * PAIRS + jj)
                    full = x_home[f, rows, lanes]
                    if size < CHUNK:
                        full = jnp.concatenate([full, jnp.zeros((CHUNK - size, 128), BF16)], axis=0)
                    mixed.append(mm(w_v[f, rows, lanes], block_pair(full)))
            for k, size in enumerate(sizes):
                rows = pl.ds(k * CHUNK, size)
                energy = square[f, rows, :]
                for jj in range(PAIRS):
                    lanes = pair_lanes(g * PAIRS + jj)
                    y = mixed[k * PAIRS + jj] + carried[k][:, jj * 128 : (jj + 1) * 128]
                    y = y + skips[pl.ds(8, 1), lanes] * x_home[f, rows, lanes].astype(F32)
                    z = z_v[f, rows, lanes].astype(F32)
                    y = y * (z * (1.0 / (1.0 + jnp.exp(-z))))
                    energy = energy + y * y
                    y_v[f, rows, pl.ds(jj * 128, 128)] = (y * gain_ref[:, lanes]).astype(BF16)
                square[f, rows, :] = energy
            return carry

        lax.fori_loop(0, frames, frame, 0)
        y_all = y_v[...].reshape(frames * seq, GROUP)
        acc[...] += mm(y_all, wz[channels(g), :])

    def advance(i, carry):
        @pl.when(jnp.logical_and(i < groups, me < holders))
        def _():
            scan_group(i)

        @pl.when(jnp.logical_and(i >= LAG, i < groups + LAG))
        def _():
            states(i - LAG)

        @pl.when(jnp.logical_and(i >= LAG + 1, i < groups + LAG + 1))
        def _():
            relay(i - LAG - 1)

        @pl.when(i >= LAG + 2)
        def _():
            finish(i - LAG - 2)

        return carry

    lax.fori_loop(0, groups + LAG + 2, advance, 0)

    def close(f, carry):
        mean = jnp.sum(square[f], axis=1, keepdims=True) * (1.0 / DI)
        scale = lax.rsqrt(mean + 1e-5)
        product = acc[pl.ds(pl.multiple_of(f * seq, 16), seq), :]
        out_ref[f] = (product * scale + tok_v[f].astype(F32)).astype(BF16)
        return carry

    lax.fori_loop(0, frames, close, 0)

    @pl.when(me < holders)
    def _():
        wait_bytes(tok_got.at[pl.ds(0, frames * (holders - 1))], tok_send)
        wait_bytes(leaving.at[:, pl.ds(0, frames * (n - 1))], ret_send)

    @pl.when(me >= holders)
    def _():
        wait_bytes(tok_got.at[pl.ds(0, frames * holders)], tok_send)

    wait_bytes(tot_got.at[others], tot_send)
    wait_bytes(end.at[:, others], st_send)
    wait_bytes(going.at[:, others], back_send)


def block(tok, w_turned, w_out, bias_t, alog_t, skip_t, bias_s, alog_s, skip_s, gain):
    n = lax.axis_size("tm")
    n_space = lax.axis_size("space")
    frames, seq = tok.shape[0], tok.shape[1]
    padded = -(-seq // CHUNK) * CHUNK
    count = padded // CHUNK
    total = n * frames
    groups = DI // GROUP
    part = frames * STATE // n_space
    tail = w_turned.shape[0] - 2 * DI
    anywhere = pl.BlockSpec(memory_space=pl.ANY)
    in_vmem = pl.BlockSpec(memory_space=pltpu.VMEM)
    dma = pltpu.SemaphoreType.DMA
    vmem = pltpu.VMEM
    return pl.pallas_call(
        functools.partial(block_kernel, n, n_space),
        out_shape=jax.ShapeDtypeStruct((frames, seq, D), BF16),
        in_specs=[anywhere] * 3 + [in_vmem] * 7,
        out_specs=in_vmem,
        scratch_shapes=[
            vmem((frames, seq, D), BF16),
            vmem((total, ITEMS, D), BF16),
            vmem((DI, D), BF16),
            vmem((DI, D), BF16),
            vmem((tail, D), BF16),
            vmem((frames, seq, DI), BF16),
            vmem((frames, padded, DI), BF16),
            vmem((PAIRS, total * ITEMS, 128), F32),
            vmem((PAIRS, total * ITEMS, 128), F32),
            vmem((PAIRS, total * ITEMS, 128), F32),
            vmem((groups, total, ITEMS, GROUP), BF16),
            vmem((2, total * ITEMS, 128), F32),
            vmem((ITEMS, 128, 128), F32),
            vmem((count, 128, 128), F32),
            vmem((ITEMS, CHUNK, 128), F32),
            vmem((ITEMS, CHUNK, 3 * HEADS), BF16),
            vmem((CHUNK, DI), F32),
            vmem((3 * HEADS, DI), BF16),
            vmem((16, DI), F32),
            vmem((frames, padded, 2 * STATE), BF16),
            vmem((frames, padded, 2 * HEADS), BF16),
            vmem((frames, padded, 3 * HEADS), BF16),
            vmem((frames, 8 * count, DI), F32),
            vmem((frames, 8 * count, DI), F32),
            vmem((frames, seq, DI), BF16),
            vmem((frames, 8, 128), F32),
            vmem((n_space, 8, 128), F32),
            vmem((n_space * 8, DI), F32),
            vmem((frames, count * STATE, DI), BF16),
            vmem((groups, n_space, part, GROUP), BF16),
            vmem((groups, n_space, part, GROUP), BF16),
            vmem((groups, n_space, part, GROUP), BF16),
            vmem((groups, n_space, part, GROUP), BF16),
            vmem((frames, seq, GROUP), BF16),
            vmem((frames, seq, 128), F32),
            vmem((frames * seq, D), F32),
            dma((5,)),
            dma(()),
            dma(()),
            dma(()),
            dma((groups,)),
            dma(()),
            dma(()),
            dma(()),
            dma((groups,)),
            dma(()),
            dma((groups,)),
        ],
        compiler_params=pltpu.CompilerParams(
            collective_id=0, has_side_effects=True, vmem_limit_bytes=60 * MIB
        ),
    )(tok, w_turned, w_out, bias_t, alog_t, skip_t, bias_s, alog_s, skip_s, gain)


def body(
    tokens,
    w_in,
    w_out,
    a_log_time,
    a_log_space,
    dt_bias_time,
    dt_bias_space,
    skip_time,
    skip_space,
    norm_gain,
):
    frames = tokens.shape[0]
    tok = tokens.reshape(frames, -1, D)
    one = lambda v: v.reshape(1, -1)
    out = block(
        tok,
        w_in.T,
        w_out,
        one(dt_bias_time),
        one(a_log_time),
        one(skip_time),
        one(dt_bias_space),
        one(a_log_space),
        one(skip_space),
        one(norm_gain),
    )
    return out.reshape(tokens.shape)


def solution(mesh):
    placed = (P("tm", "space", None, None), P(), P(), P(), P(), P(), P(), P(), P(), P())
    return jax.shard_map(
        body, mesh=mesh, in_specs=placed, out_specs=P("tm", "space", None, None), check_vma=False
    )
```

time: 1100 us -> 128 us (0.12); the launches traced: 1080 us -> 128 us
  waiting for transfers between devices: 687 us -> 0 us
  local copies, waits for them, and re-layouts: 161 us -> 2.97 us
  Pallas kernels: 0 us -> 125 us
  matrix products: 105 us -> 0 us
  other arithmetic: 66.9 us -> 0 us
  starting transfers between devices: 62.1 us -> 0 us
    ppermute x7 -> x0, waiting for transfers between devices: 598 us -> none  [from_behind(): lax.ppermute(value, axis, [(source, source + steps) for source in range(l...]
    pallas_call x0 -> x1, Pallas kernels: none -> 125 us  [block(): pl.pallas_call(functools.partial(block_kernel, n, n_space), out_shape=jax...]
    dot_general x20 -> x0, matrix products: 105 us -> none  [the longest x4 42.1 us: local_scan(): jnp.einsum('srh,rhp->shp', weights, signal, precision=lax.Precision.HIGHEST)]
    all_to_all x2 -> x0, waiting for transfers between devices: 89 us -> none  [the longest x1 54.7 us: body(): lax.all_to_all(sending, 'tm', split_axis=1, concat_axis=0, tiled=True)]
    reshape x5 -> x0, local copies, waits for them, and re-layouts: 62.9 us -> none  [the longest x1 23.2 us: body(): space_in = time_out.reshape(fr_dev, rows_dev, cols_dev, HEADS, HEAD_DIM)]
    ppermute x7 -> x0, starting transfers between devices: 47.3 us -> none  [from_behind(): lax.ppermute(value, axis, [(source, source + steps) for source in range(l...]
    add x7 -> x0, other arithmetic: 41.3 us -> none  [relay_step(): return from_behind(growth * start_state + end_state, 'space', 1)]
    slice x9 -> x0, local copies, waits for them, and re-layouts: 22 us -> none  [the longest x1 7.02 us: body(): inner_seq = sequences[..., :DI].reshape(item_count, frames, HEADS, HEAD_DIM)]
  transfers between devices with their start and end apart: 9 -> 0, of which waited for: 9 -> 0; matrix products, arithmetic and copies ran while one was open for 2% -> 0% of each run, Pallas kernels for 0% -> 0%
where the time goes in v3:
time: 128 us
  Pallas kernels  125 us (98%)
  local copies, waits for them, and re-layouts  2.97 us (2%)
    pallas_call x1, Pallas kernels, block(): pl.pallas_call(functools.partial(block_kernel, n, n_space), out_shape=jax...  125 us
    unnamed x1, local copies, waits for them, and re-layouts  2.97 us

profile of v3, /device:TPU:0, one launch (start us, length us, event | category | flops | bytes accessed | tf_op | source)
XLA Modules:
  0.0 127.8 jit_solution(10813387731379334926)
XLA Ops:
  0.0 124.8 %shard_map.100 = bf16[4,240,1024]{2,1,0:T(8,128)(2,1)} custom-call(bf16[4,240,1024]{2,1,0:T(8,128)(2,1)} %bitcast.12, bf16[4416,1024]{1,0:T(8,128)(2,1)} %bitcast.10, bf16[2048,1024]{1,0:T(8,128)(2,1)} %wo_hbm.1, f32[1,32]{1,0:T(1,128)} %bitcast.14, f32[1,32]{1,0:T(1,128)} %bitcast.15, f32[1,32]{1,0:T(1,128)} %bitcast.16, f32[1,32]{1,0:T(1,128)} %bitcast.17, ...), custom_call_target="tpu_custom_call" | custom-call | tf_op jit(solution)/shard_map/pallas_call | solution.py:569
  124.8 3.0 %copy.12 = bf16[4,3,80,1024]{3,2,1,0:T(8,128)(2,1)} copy(bf16[4,3,80,1024]{3,2,1,0:T(8,128)(2,1)} %bitcast.11) | data formatting | bytes 3932160

commit v4 on v3

--- a/solution.py
+++ b/solution.py
@@ -83,10 +83,12 @@
 
 
 ITEMS = 16
-GROUP = 256
+GROUP = 512
 PAIRS = GROUP // 128
 TOGETHER = 4
-LAG = 1
+LAG = 2
+HALF = 8
+ROUNDS = ITEMS // HALF
 
 
 def nt(a, b):
@@ -202,9 +204,6 @@
             device_id_type=pl.DeviceIdType.MESH,
         )
 
-    def positions(d):
-        return pl.ds(pl.multiple_of(d * ITEMS, ITEMS), ITEMS)
-
     def frame_rows(d):
         return pl.ds(d * frames, frames)
 
@@ -214,34 +213,40 @@
     def pair_lanes(j):
         return pl.ds(pl.multiple_of(j * 128, 128), 128)
 
-    def tok_copy(d, source):
+    def block_of(d, h):
+        return pl.ds(pl.multiple_of(d * ITEMS + h * HALF, HALF), HALF)
+
+    def tok_copy(d, source, h):
         return remote(
-            tok_hbm.at[:, positions(d), :],
-            tok_got.at[frame_rows(source)],
+            tok_hbm.at[:, block_of(d, h), :],
+            tok_got.at[h, frame_rows(source)],
             tok_send,
-            tok_recv,
+            tok_recv.at[h],
             "tm",
             d,
         )
 
-    def ret_copy(d, source, g):
+    def ret_copy(d, source, g, h):
         return remote(
-            leaving.at[g, frame_rows(d)],
-            x_home.at[:, positions(source), channels(g)],
+            leaving.at[h, g, frame_rows(d)],
+            x_home.at[:, block_of(source, h), channels(g)],
             ret_send,
             ret_recv.at[g],
             "tm",
             d,
         )
 
-    def own_copy(g):
+    def own_copy(g, h):
         return pltpu.make_async_copy(
-            leaving.at[g, frame_rows(me)], x_home.at[:, positions(me), channels(g)], ret_recv.at[g]
-        )
-
-    own_tok = pltpu.make_async_copy(
-        tok_hbm.at[:, positions(lax.rem(me, holders)), :], tok_got.at[frame_rows(me)], tok_recv
-    )
+            leaving.at[h, g, frame_rows(me)], x_home.at[:, block_of(me, h), channels(g)], ret_recv.at[g]
+        )
+
+    def own_tok(h):
+        return pltpu.make_async_copy(
+            tok_hbm.at[:, block_of(lax.rem(me, holders), h), :],
+            tok_got.at[h, frame_rows(me)],
+            tok_recv.at[h],
+        )
 
     def tot_copy(s, slot):
         return remote(
@@ -279,20 +284,22 @@
         )
     pl.semaphore_wait(barrier, n + n_space - 2)
 
-    def send_tokens(step, carry):
-        d = lax.rem(me + step, n)
+    def send_tokens(i, carry):
+        h = i // (n - 1)
+        d = lax.rem(me + 1 + lax.rem(i, n - 1), n)
 
         @pl.when(d < holders)
         def _():
-            tok_copy(d, me).start()
+            tok_copy(d, me, h).start()
 
         return carry
 
-    lax.fori_loop(1, n, send_tokens, 0)
+    lax.fori_loop(0, ROUNDS * (n - 1), send_tokens, 0)
 
     @pl.when(me < holders)
     def _():
-        own_tok.start()
+        for h in range(ROUNDS):
+            own_tok(h).start()
 
     spread[...] = head_spread()
     skips[...] = widen(
@@ -361,19 +368,18 @@
     wo_load.start()
     wx_load.wait()
 
-    @pl.when(me < holders)
-    def _():
-        wait_bytes(tok_got, tok_recv)
-        tail = rounded(nt(tok_got[...].reshape(total * ITEMS, D), wt[...]))
+    def prepare_round(h):
+        wait_bytes(tok_got.at[h], tok_recv.at[h])
+        tail = rounded(nt(tok_got[h].reshape(total * HALF, D), wt[...]))
         small_t[0] = tail[:, : 2 * STATE]
         small_t[1] = jnp.concatenate(
-            [tail[:, 4 * STATE :], jnp.zeros((total * ITEMS, 128 - 2 * HEADS), F32)], axis=1
+            [tail[:, 4 * STATE :], jnp.zeros((total * HALF, 128 - 2 * HEADS), F32)], axis=1
         )
         rate = -jnp.exp(alog_t_ref[...])
 
         def prepare(q, carry):
             several = [q * TOGETHER + u for u in range(TOGETHER)]
-            rows = [pl.ds(p, CHUNK, stride=ITEMS) for p in several]
+            rows = [pl.ds(p, CHUNK, stride=HALF) for p in several]
             pairs = [small_t[0, r, :].astype(BF16) for r in rows]
             steps = [softplus(small_t[1, r, :][:, :HEADS] + bias_t_ref[...]) for r in rows]
             scores = [masked_scores(pair[:, STATE:], pair[:, :STATE]) for pair in pairs]
@@ -385,16 +391,17 @@
                 cum3[p] = split3(cums[u])
             return carry
 
-        lax.fori_loop(0, ITEMS // TOGETHER, prepare, 0)
-
-    wait_bytes(tot_got.at[others], tot_recv)
-    totals = jnp.concatenate([tot_got[s] for s in range(n_space)], axis=0)[:, :HEADS]
-    growth[...] = widen(jnp.exp(totals), spread)
-    wo_load.wait()
-
-    def scan_group(g):
-        x = rounded(nt(tok_got[...].reshape(total * ITEMS, D), wx[channels(g), :]))
-        cum = mm(cum3[...].reshape(ITEMS * CHUNK, 3 * HEADS), spread[:, channels(g)])
+        lax.fori_loop(0, HALF // TOGETHER, prepare, 0)
+
+    def take_totals():
+        wait_bytes(tot_got.at[others], tot_recv)
+        totals = jnp.concatenate([tot_got[s] for s in range(n_space)], axis=0)[:, :HEADS]
+        growth[...] = widen(jnp.exp(totals), spread)
+        wo_load.wait()
+
+    def scan_group(g, h):
+        x = rounded(nt(tok_got[h].reshape(total * HALF, D), wx[channels(g), :]))
+        cum = mm(cum3[...].reshape(HALF * CHUNK, 3 * HEADS), spread[:, channels(g)])
         for jj in range(PAIRS):
             x_group[jj] = x[:, jj * 128 : (jj + 1) * 128]
             cum_group[jj] = cum[:, jj * 128 : (jj + 1) * 128]
@@ -411,25 +418,25 @@
                 )
                 for p, jj in work
             ]
-            inputs = [x_group[jj, pl.ds(p, CHUNK, stride=ITEMS), :] for p, jj in work]
+            inputs = [x_group[jj, pl.ds(p, CHUNK, stride=HALF), :] for p, jj in work]
             mixed = [mm(w, block_pair(x.astype(BF16))) for w, x in zip(weights, inputs)]
             for u, (p, jj) in enumerate(work):
                 skip = skips[pl.ds(0, 1), pair_lanes(g * PAIRS + jj)]
-                out_group[jj, pl.ds(p, CHUNK, stride=ITEMS), :] = mixed[u] + skip * inputs[u]
+                out_group[jj, pl.ds(p, CHUNK, stride=HALF), :] = mixed[u] + skip * inputs[u]
             return inner
 
-        lax.fori_loop(0, ITEMS // TOGETHER, item, 0)
+        lax.fori_loop(0, HALF // TOGETHER, item, 0)
         for jj in range(PAIRS):
-            leaving[g, :, :, pl.ds(jj * 128, 128)] = (
-                out_group[jj].astype(BF16).reshape(total, ITEMS, 128)
+            leaving[h, g, :, :, pl.ds(jj * 128, 128)] = (
+                out_group[jj].astype(BF16).reshape(total, HALF, 128)
             )
 
         def send(step, inner):
-            ret_copy(lax.rem(me + step, n), me, g).start()
+            ret_copy(lax.rem(me + step, n), me, g, h).start()
             return inner
 
         lax.fori_loop(1, n, send, 0)
-        own_copy(g).start()
+        own_copy(g, h).start()
 
     def states(g):
         wait_bytes(x_home.at[:, :, channels(g)], ret_recv.at[g])
@@ -508,26 +515,40 @@
         y_all = y_v[...].reshape(frames * seq, GROUP)
         acc[...] += mm(y_all, wz[channels(g), :])
 
+    first = (ROUNDS - 1) * groups + LAG
+
     def advance(i, carry):
-        @pl.when(jnp.logical_and(i < groups, me < holders))
+        g = lax.rem(i, groups)
+        h = i // groups
+        scanning = jnp.logical_and(i < ROUNDS * groups, me < holders)
+
+        @pl.when(jnp.logical_and(scanning, g == 0))
         def _():
-            scan_group(i)
-
-        @pl.when(jnp.logical_and(i >= LAG, i < groups + LAG))
+            prepare_round(h)
+
+        @pl.when(scanning)
         def _():
-            states(i - LAG)
-
-        @pl.when(jnp.logical_and(i >= LAG + 1, i < groups + LAG + 1))
+            scan_group(g, h)
+
+        @pl.when(i == first)
         def _():
-            relay(i - LAG - 1)
-
-        @pl.when(i >= LAG + 2)
+            take_totals()
+
+        @pl.when(jnp.logical_and(i >= first, i < first + groups))
         def _():
-            finish(i - LAG - 2)
+            states(i - first)
+
+        @pl.when(jnp.logical_and(i >= first + 1, i < first + 1 + groups))
+        def _():
+            relay(i - first - 1)
+
+        @pl.when(i >= first + 2)
+        def _():
+            finish(i - first - 2)
 
         return carry
 
-    lax.fori_loop(0, groups + LAG + 2, advance, 0)
+    lax.fori_loop(0, first + 2 + groups, advance, 0)
 
     def close(f, carry):
         mean = jnp.sum(square[f], axis=1, keepdims=True) * (1.0 / DI)
@@ -540,12 +561,12 @@
 
     @pl.when(me < holders)
     def _():
-        wait_bytes(tok_got.at[pl.ds(0, frames * (holders - 1))], tok_send)
-        wait_bytes(leaving.at[:, pl.ds(0, frames * (n - 1))], ret_send)
+        wait_bytes(tok_got.at[:, pl.ds(0, frames * (holders - 1))], tok_send)
+        wait_bytes(leaving.at[:, :, pl.ds(0, frames * (n - 1))], ret_send)
 
     @pl.when(me >= holders)
     def _():
-        wait_bytes(tok_got.at[pl.ds(0, frames * holders)], tok_send)
+        wait_bytes(tok_got.at[:, pl.ds(0, frames * holders)], tok_send)
 
     wait_bytes(tot_got.at[others], tot_send)
     wait_bytes(end.at[:, others], st_send)
@@ -573,21 +594,21 @@
         out_specs=in_vmem,
         scratch_shapes=[
             vmem((frames, seq, D), BF16),
-            vmem((total, ITEMS, D), BF16),
+            vmem((ROUNDS, total, HALF, D), BF16),
             vmem((DI, D), BF16),
             vmem((DI, D), BF16),
             vmem((tail, D), BF16),
             vmem((frames, seq, DI), BF16),
             vmem((frames, padded, DI), BF16),
-            vmem((PAIRS, total * ITEMS, 128), F32),
-            vmem((PAIRS, total * ITEMS, 128), F32),
-            vmem((PAIRS, total * ITEMS, 128), F32),
-            vmem((groups, total, ITEMS, GROUP), BF16),
-            vmem((2, total * ITEMS, 128), F32),
-            vmem((ITEMS, 128, 128), F32),
+            vmem((PAIRS, total * HALF, 128), F32),
+            vmem((PAIRS, total * HALF, 128), F32),
+            vmem((PAIRS, total * HALF, 128), F32),
+            vmem((ROUNDS, groups, total, HALF, GROUP), BF16),
+            vmem((2, total * HALF, 128), F32),
+            vmem((HALF, 128, 128), F32),
             vmem((count, 128, 128), F32),
-            vmem((ITEMS, CHUNK, 128), F32),
-            vmem((ITEMS, CHUNK, 3 * HEADS), BF16),
+            vmem((HALF, CHUNK, 128), F32),
+            vmem((HALF, CHUNK, 3 * HEADS), BF16),
             vmem((CHUNK, DI), F32),
             vmem((3 * HEADS, DI), BF16),
             vmem((16, DI), F32),
@@ -610,7 +631,7 @@
             vmem((frames * seq, D), F32),
             dma((5,)),
             dma(()),
-            dma(()),
+            dma((ROUNDS,)),
             dma(()),
             dma((groups,)),
             dma(()),

time: 128 us -> 117 us (0.914)
  Pallas kernels: 125 us -> 113 us
    pallas_call x1, Pallas kernels: 125 us -> 113 us  [block(): pl.pallas_call(functools.partial(block_kernel, n, n_space), out_shape=jax...]
where the time goes in v4:
time: 117 us; the launch traced here: 116 us
  Pallas kernels  113 us (97%)
  local copies, waits for them, and re-layouts  2.97 us (3%)
    pallas_call x1, Pallas kernels, block(): pl.pallas_call(functools.partial(block_kernel, n, n_space), out_shape=jax...  113 us
    unnamed x1, local copies, waits for them, and re-layouts  2.97 us

profile of v4, /device:TPU:0, one launch (start us, length us, event | category | flops | bytes accessed | tf_op | source)
XLA Modules:
  0.0 116.2 jit_solution(8371539196739242757)
XLA Ops:
  0.0 113.2 %shard_map.100 = bf16[4,240,1024]{2,1,0:T(8,128)(2,1)} custom-call(bf16[4,240,1024]{2,1,0:T(8,128)(2,1)} %bitcast.12, bf16[4416,1024]{1,0:T(8,128)(2,1)} %bitcast.10, bf16[2048,1024]{1,0:T(8,128)(2,1)} %wo_hbm.1, f32[1,32]{1,0:T(1,128)} %bitcast.14, f32[1,32]{1,0:T(1,128)} %bitcast.15, f32[1,32]{1,0:T(1,128)} %bitcast.16, f32[1,32]{1,0:T(1,128)} %bitcast.17, ...), custom_call_target="tpu_custom_call" | custom-call | tf_op jit(solution)/shard_map/pallas_call | solution.py:590
  113.3 3.0 %copy.12 = bf16[4,3,80,1024]{3,2,1,0:T(8,128)(2,1)} copy(bf16[4,3,80,1024]{3,2,1,0:T(8,128)(2,1)} %bitcast.11) | data formatting | bytes 3932160

commit v5 on v4

--- a/solution.py
+++ b/solution.py
@@ -86,7 +86,10 @@
 GROUP = 512
 PAIRS = GROUP // 128
 TOGETHER = 4
-LAG = 2
+NARROW = 256
+RELAY_LAG = 2
+FINISH_LAG = 4
+NPAIRS = NARROW // 128
 HALF = 8
 ROUNDS = ITEMS // HALF
 
@@ -179,6 +182,7 @@
     holders = seq // ITEMS
     total = n * frames
     groups = DI // GROUP
+    narrow_groups = DI // NARROW
     halves = n_space // frames
     part = STATE // halves
     me = lax.axis_index("tm")
@@ -209,6 +213,9 @@
 
     def channels(g):
         return pl.ds(pl.multiple_of(g * GROUP, GROUP), GROUP)
+
+    def narrow(g):
+        return pl.ds(pl.multiple_of(g * NARROW, NARROW), NARROW)
 
     def pair_lanes(j):
         return pl.ds(pl.multiple_of(j * 128, 128), 128)
@@ -439,19 +446,24 @@
         own_copy(g, h).start()
 
     def states(g):
-        wait_bytes(x_home.at[:, :, channels(g)], ret_recv.at[g])
+        whole = lax.div(g, GROUP // NARROW)
+
+        @pl.when(lax.rem(g, GROUP // NARROW) == 0)
+        def _():
+            wait_bytes(x_home.at[:, :, channels(whole)], ret_recv.at[whole])
+
         pieces = [(f, k, min(CHUNK, seq - k * CHUNK)) for f in range(frames) for k in range(count)]
         added = []
         for f, k, size in pieces:
             rows = pl.ds(k * CHUNK, size)
-            tail_wide = mm(tail_s[f, rows, :], spread[: 2 * HEADS, channels(g)])
-            weighted = (x_home[f, rows, channels(g)].astype(F32) * tail_wide).astype(BF16)
+            tail_wide = mm(tail_s[f, rows, :], spread[: 2 * HEADS, narrow(g)])
+            weighted = (x_home[f, rows, narrow(g)].astype(F32) * tail_wide).astype(BF16)
             added.append(tn(small_s[f, rows, :STATE], weighted))
         for f in range(frames):
-            state = jnp.zeros((STATE, GROUP), F32)
+            state = jnp.zeros((STATE, NARROW), F32)
             for k in range(count):
-                starts[f, pl.ds(k * STATE, STATE), channels(g)] = state.astype(BF16)
-                state = rate_s[f, pl.ds(8 * k, 1), channels(g)] * state + added[f * count + k]
+                starts[f, pl.ds(k * STATE, STATE), narrow(g)] = state.astype(BF16)
+                state = rate_s[f, pl.ds(8 * k, 1), narrow(g)] * state + added[f * count + k]
             for half in range(halves):
                 end[g, halves * f + half] = state[half * part : (half + 1) * part].astype(BF16)
 
@@ -464,10 +476,10 @@
 
     def relay(g):
         wait_bytes(got.at[g, others], st_recv.at[g])
-        running = jnp.zeros((part, GROUP), F32)
+        running = jnp.zeros((part, NARROW), F32)
         for s in range(n_space):
             going[g, s] = running.astype(BF16)
-            running = growth[pl.ds(8 * s, 1), channels(g)] * running + got[g, s].astype(F32)
+            running = growth[pl.ds(8 * s, 1), narrow(g)] * running + got[g, s].astype(F32)
 
         def send_back(step, carry):
             back_copy(lax.rem(here + step, n_space), here, g).start()
@@ -487,12 +499,12 @@
             carried, mixed = [], []
             for k, size in enumerate(sizes):
                 rows = pl.ds(k * CHUNK, size)
-                reach = reach_s[f, pl.ds(8 * k, 1), channels(g)]
-                state = starts[f, pl.ds(k * STATE, STATE), channels(g)].astype(F32) + reach * arrived
+                reach = reach_s[f, pl.ds(8 * k, 1), narrow(g)]
+                state = starts[f, pl.ds(k * STATE, STATE), narrow(g)].astype(F32) + reach * arrived
                 product = mm(small_s[f, rows, STATE:], state.astype(BF16))
-                carried.append(product * mm(grown_s[f, rows, :], spread[:, channels(g)]))
-                for jj in range(PAIRS):
-                    lanes = pair_lanes(g * PAIRS + jj)
+                carried.append(product * mm(grown_s[f, rows, :], spread[:, narrow(g)]))
+                for jj in range(NPAIRS):
+                    lanes = pair_lanes(g * NPAIRS + jj)
                     full = x_home[f, rows, lanes]
                     if size < CHUNK:
                         full = jnp.concatenate([full, jnp.zeros((CHUNK - size, 128), BF16)], axis=0)
@@ -500,9 +512,9 @@
             for k, size in enumerate(sizes):
                 rows = pl.ds(k * CHUNK, size)
                 energy = square[f, rows, :]
-                for jj in range(PAIRS):
-                    lanes = pair_lanes(g * PAIRS + jj)
-                    y = mixed[k * PAIRS + jj] + carried[k][:, jj * 128 : (jj + 1) * 128]
+                for jj in range(NPAIRS):
+                    lanes = pair_lanes(g * NPAIRS + jj)
+                    y = mixed[k * NPAIRS + jj] + carried[k][:, jj * 128 : (jj + 1) * 128]
                     y = y + skips[pl.ds(8, 1), lanes] * x_home[f, rows, lanes].astype(F32)
                     z = z_v[f, rows, lanes].astype(F32)
                     y = y * (z * (1.0 / (1.0 + jnp.exp(-z))))
@@ -512,43 +524,42 @@
             return carry
 
         lax.fori_loop(0, frames, frame, 0)
-        y_all = y_v[...].reshape(frames * seq, GROUP)
-        acc[...] += mm(y_all, wz[channels(g), :])
-
-    first = (ROUNDS - 1) * groups + LAG
+        y_all = y_v[...].reshape(frames * seq, NARROW)
+        acc[...] += mm(y_all, wz[narrow(g), :])
+
+    @pl.when(me < holders)
+    def _():
+        def scan(i, carry):
+            g = lax.rem(i, groups)
+            h = i // groups
+
+            @pl.when(g == 0)
+            def _():
+                prepare_round(h)
+
+            scan_group(g, h)
+            return carry
+
+        lax.fori_loop(0, ROUNDS * groups, scan, 0)
+
+    take_totals()
 
     def advance(i, carry):
-        g = lax.rem(i, groups)
-        h = i // groups
-        scanning = jnp.logical_and(i < ROUNDS * groups, me < holders)
-
-        @pl.when(jnp.logical_and(scanning, g == 0))
+        @pl.when(i < narrow_groups)
         def _():
-            prepare_round(h)
-
-        @pl.when(scanning)
+            states(i)
+
+        @pl.when(jnp.logical_and(i >= RELAY_LAG, i < narrow_groups + RELAY_LAG))
         def _():
-            scan_group(g, h)
-
-        @pl.when(i == first)
+            relay(i - RELAY_LAG)
+
+        @pl.when(i >= FINISH_LAG)
         def _():
-            take_totals()
-
-        @pl.when(jnp.logical_and(i >= first, i < first + groups))
-        def _():
-            states(i - first)
-
-        @pl.when(jnp.logical_and(i >= first + 1, i < first + 1 + groups))
-        def _():
-            relay(i - first - 1)
-
-        @pl.when(i >= first + 2)
-        def _():
-            finish(i - first - 2)
+            finish(i - FINISH_LAG)
 
         return carry
 
-    lax.fori_loop(0, first + 2 + groups, advance, 0)
+    lax.fori_loop(0, narrow_groups + FINISH_LAG, advance, 0)
 
     def close(f, carry):
         mean = jnp.sum(square[f], axis=1, keepdims=True) * (1.0 / DI)
@@ -622,11 +633,11 @@
             vmem((n_space, 8, 128), F32),
             vmem((n_space * 8, DI), F32),
             vmem((frames, count * STATE, DI), BF16),
-            vmem((groups, n_space, part, GROUP), BF16),
-            vmem((groups, n_space, part, GROUP), BF16),
-            vmem((groups, n_space, part, GROUP), BF16),
-            vmem((groups, n_space, part, GROUP), BF16),
-            vmem((frames, seq, GROUP), BF16),
+            vmem((DI // NARROW, n_space, part, NARROW), BF16),
+            vmem((DI // NARROW, n_space, part, NARROW), BF16),
+            vmem((DI // NARROW, n_space, part, NARROW), BF16),
+            vmem((DI // NARROW, n_space, part, NARROW), BF16),
+            vmem((frames, seq, NARROW), BF16),
             vmem((frames, seq, 128), F32),
             vmem((frames * seq, D), F32),
             dma((5,)),
@@ -637,9 +648,9 @@
             dma(()),
             dma(()),
             dma(()),
-            dma((groups,)),
+            dma((DI // NARROW,)),
             dma(()),
-            dma((groups,)),
+            dma((DI // NARROW,)),
         ],
         compiler_params=pltpu.CompilerParams(
             collective_id=0, has_side_effects=True, vmem_limit_bytes=60 * MIB

time: 117 us -> 113 us (0.966)
  Pallas kernels: 113 us -> 110 us
    pallas_call x1, Pallas kernels: 113 us -> 110 us  [block(): pl.pallas_call(functools.partial(block_kernel, n, n_space), out_shape=jax...]
where the time goes in v5:
time: 113 us
  Pallas kernels  110 us (97%)
  local copies, waits for them, and re-layouts  2.97 us (3%)
    pallas_call x1, Pallas kernels, block(): pl.pallas_call(functools.partial(block_kernel, n, n_space), out_shape=jax...  110 us
    unnamed x1, local copies, waits for them, and re-layouts  2.97 us

profile of v5, /device:TPU:0, one launch (start us, length us, event | category | flops | bytes accessed | tf_op | source)
XLA Modules:
  0.0 113.0 jit_solution(14898919362621439121)
XLA Ops:
  0.0 110.0 %shard_map.100 = bf16[4,240,1024]{2,1,0:T(8,128)(2,1)} custom-call(bf16[4,240,1024]{2,1,0:T(8,128)(2,1)} %bitcast.12, bf16[4416,1024]{1,0:T(8,128)(2,1)} %bitcast.10, bf16[2048,1024]{1,0:T(8,128)(2,1)} %wo_hbm.1, f32[1,32]{1,0:T(1,128)} %bitcast.14, f32[1,32]{1,0:T(1,128)} %bitcast.15, f32[1,32]{1,0:T(1,128)} %bitcast.16, f32[1,32]{1,0:T(1,128)} %bitcast.17, ...), custom_call_target="tpu_custom_call" | custom-call | tf_op jit(solution)/shard_map/pallas_call | solution.py:601
  110.0 3.0 %copy.12 = bf16[4,3,80,1024]{3,2,1,0:T(8,128)(2,1)} copy(bf16[4,3,80,1024]{3,2,1,0:T(8,128)(2,1)} %bitcast.11) | data formatting | bytes 3932160

commit v6 on v5

--- a/solution.py
+++ b/solution.py
@@ -491,7 +491,7 @@
     def finish(g):
         wait_bytes(entering.at[g, others], back_recv.at[g])
 
-        def frame(f, carry):
+        def frame(f):
             arrived = jnp.concatenate(
                 [entering[g, halves * f + half] for half in range(halves)], axis=0
             ).astype(F32)
@@ -521,9 +521,9 @@
                     energy = energy + y * y
                     y_v[f, rows, pl.ds(jj * 128, 128)] = (y * gain_ref[:, lanes]).astype(BF16)
                 square[f, rows, :] = energy
-            return carry
-
-        lax.fori_loop(0, frames, frame, 0)
+
+        for f in range(frames):
+            frame(f)
         y_all = y_v[...].reshape(frames * seq, NARROW)
         acc[...] += mm(y_all, wz[narrow(g), :])
 

time: 113 us -> 112 us (level)
    pallas_call x1, Pallas kernels: 110 us -> 109 us  [block(): pl.pallas_call(functools.partial(block_kernel, n, n_space), out_shape=jax...]
where the time goes in v6:
time: 112 us
  Pallas kernels  109 us (97%)
  local copies, waits for them, and re-layouts  2.97 us (3%)
    pallas_call x1, Pallas kernels, block(): pl.pallas_call(functools.partial(block_kernel, n, n_space), out_shape=jax...  109 us
    unnamed x1, local copies, waits for them, and re-layouts  2.97 us

profile of v6, /device:TPU:0, one launch (start us, length us, event | category | flops | bytes accessed | tf_op | source)
XLA Modules:
  0.0 111.7 jit_solution(7058600447870978)
XLA Ops:
  0.0 108.7 %shard_map.100 = bf16[4,240,1024]{2,1,0:T(8,128)(2,1)} custom-call(bf16[4,240,1024]{2,1,0:T(8,128)(2,1)} %bitcast.12, bf16[4416,1024]{1,0:T(8,128)(2,1)} %bitcast.10, bf16[2048,1024]{1,0:T(8,128)(2,1)} %wo_hbm.1, f32[1,32]{1,0:T(1,128)} %bitcast.14, f32[1,32]{1,0:T(1,128)} %bitcast.15, f32[1,32]{1,0:T(1,128)} %bitcast.16, f32[1,32]{1,0:T(1,128)} %bitcast.17, ...), custom_call_target="tpu_custom_call" | custom-call | tf_op jit(solution)/shard_map/pallas_call | solution.py:601
  108.7 3.0 %copy.12 = bf16[4,3,80,1024]{3,2,1,0:T(8,128)(2,1)} copy(bf16[4,3,80,1024]{3,2,1,0:T(8,128)(2,1)} %bitcast.11) | data formatting | bytes 3932160

commit v7 on v6

--- a/solution.py
+++ b/solution.py
@@ -83,9 +83,9 @@
 
 
 ITEMS = 16
-GROUP = 512
+GROUP = 256
 PAIRS = GROUP // 128
-TOGETHER = 4
+TOGETHER = 8
 NARROW = 256
 RELAY_LAG = 2
 FINISH_LAG = 4

time: 112 us -> 112 us (level)
  no operation moved by 1% of the time
where the time goes in v7:
time: 112 us
  Pallas kernels  109 us (97%)
  local copies, waits for them, and re-layouts  2.97 us (3%)
    pallas_call x1, Pallas kernels, block(): pl.pallas_call(functools.partial(block_kernel, n, n_space), out_shape=jax...  109 us
    unnamed x1, local copies, waits for them, and re-layouts  2.97 us

profile of v7, /device:TPU:0, one launch (start us, length us, event | category | flops | bytes accessed | tf_op | source)
XLA Modules:
  0.0 111.8 jit_solution(897833153229723876)
XLA Ops:
  0.0 108.8 %shard_map.100 = bf16[4,240,1024]{2,1,0:T(8,128)(2,1)} custom-call(bf16[4,240,1024]{2,1,0:T(8,128)(2,1)} %bitcast.12, bf16[4416,1024]{1,0:T(8,128)(2,1)} %bitcast.10, bf16[2048,1024]{1,0:T(8,128)(2,1)} %wo_hbm.1, f32[1,32]{1,0:T(1,128)} %bitcast.14, f32[1,32]{1,0:T(1,128)} %bitcast.15, f32[1,32]{1,0:T(1,128)} %bitcast.16, f32[1,32]{1,0:T(1,128)} %bitcast.17, ...), custom_call_target="tpu_custom_call" | custom-call | tf_op jit(solution)/shard_map/pallas_call | solution.py:601
  108.9 3.0 %copy.12 = bf16[4,3,80,1024]{3,2,1,0:T(8,128)(2,1)} copy(bf16[4,3,80,1024]{3,2,1,0:T(8,128)(2,1)} %bitcast.11) | data formatting | bytes 3932160
